TPU v7x, 32 devices: a whole 2x2x4 slice. The times are simulated.
32 devices in a mesh: groups: 2 (over y), seq: 4 (over z), head: 2 (over x), sub: 2 (over core).
Axes of the slice: x: 2, y: 2, z: 4, core: 2. Of those that a mesh axis runs over, the one named last changes fastest.
Arguments:
- frames_in: bfloat16 [2048, 1536], P(('groups', 'seq', 'head', 'sub')), parts along dimension 0, may hold values from -30 to 30
- attn_gain: float32 [1536], replicated, may hold values from 0.25 to 1.75
- w_qkv: bfloat16 [1536, 24, 192], P(None, ('head', 'sub')), may hold values from -1 to 1
- w_out: bfloat16 [1536, 1536], P(('head', 'sub')), may hold values from -0.3125 to 0.3125
- vit_gain: float32 [1536], replicated, may hold values from 0.25 to 1.75
- w_pair: bfloat16 [2, 1536, 1024], P(None, None, ('head', 'sub')), may hold values from -0.109375 to 0.109375
- w_act: float32 [1024, 7], P(('head', 'sub')), may hold values from -0.375 to 0.375
- pair_frames: int32 [4, 15], P('groups'), parts along dimension 0, may hold values from 0 to 14, each once within a row
Outputs:
- hidden: bfloat16 [2048, 1536], P(('groups', 'seq', 'head', 'sub')), parts along dimension 0
- actions: float32 [4, 15, 7], P('groups'), parts along dimension 0
There are 2 independent parts, one for each index of `groups`. A program takes and returns all parts, laid end to end along the dimension named above; an argument that names none is the same for every part. Nothing has to cross between parts.
All inputs are finite; a program needn't handle non-finite values.
Results may differ from a plain program's by a relative error of at most 0.01.
Values may be sent and summed in bfloat16 or wider, within the bound.
No kernel may reach another device: no remote copies, remote signals or barrier semaphores. Data moves between devices by JAX's collectives and lax.ppermute only.
A program may use at most 64 MiB of HBM per device.

v0:
```python
import functools

import jax
import jax.numpy as jnp
from jax import lax
from jax.experimental import pallas as pl
from jax.experimental.pallas import tpu as pltpu
from jax.sharding import PartitionSpec as P


F = 16
ROLLS = 2
EPS = 1e-06
LINES = 8


def from_behind(value, axis, steps):
    count = lax.axis_size(axis)
    leading, last = (max(0, -steps), min(count, count - steps))
    return lax.ppermute(value, axis, [(source, source + steps) for source in range(leading, last)])


def normalize(values_in, gain_vec):
    floats = values_in.astype(jnp.float32)
    mean_sq = jnp.mean(floats * floats, axis=-1, keepdims=True)
    return (floats * lax.rsqrt(mean_sq + 1e-06) * gain_vec).astype(jnp.bfloat16)


def general_shards(frames_in, attn_gain, w_qkv, w_out, vit_gain, w_pair, w_act, pair_frames):
    rows_own = frames_in.shape[0]
    model_width = frames_in.shape[1]
    seq_count = lax.axis_size("seq")
    split_count = lax.axis_size(("head", "sub"))
    block_rows = rows_own * split_count
    total_cols = block_rows * seq_count // F
    frames_local = max(1, F // seq_count)
    cols_local = block_rows // frames_local
    frame_step = max(1, seq_count // F)
    heads_local = w_qkv.shape[1]
    triple_dim = w_qkv.shape[2]
    head_dim = triple_dim // 3
    qkv_matrix = w_qkv.reshape(model_width, heads_local * triple_dim)
    normed = lax.all_gather(normalize(frames_in, attn_gain), ("head", "sub"), axis=0, tiled=True)
    qkv_rows = jnp.dot(normed, qkv_matrix, preferred_element_type=jnp.float32).astype(jnp.bfloat16)
    qkv_rows = qkv_rows.reshape(
        frames_local, seq_count, cols_local // seq_count, heads_local, triple_dim
    )
    columns = lax.all_to_all(qkv_rows, "seq", split_axis=1, concat_axis=0, tiled=True)
    item_count = columns.shape[2]
    by_frame = columns.reshape(F, -1, heads_local, triple_dim)
    queries = by_frame[..., :head_dim]
    key_part = by_frame[..., head_dim : 2 * head_dim]
    value_part = by_frame[..., 2 * head_dim :]
    scores = jnp.einsum(
        "fchd,gchd->chfg", queries, key_part, preferred_element_type=jnp.float32
    ) * head_dim ** (-0.5)
    row_peak = jnp.max(scores, axis=-1, keepdims=True)
    weights = jnp.exp(scores - row_peak)
    weights = (weights / jnp.sum(weights, axis=-1, keepdims=True)).astype(jnp.bfloat16)
    mixed_out = jnp.einsum(
        "chfg,gchd->fchd", weights, value_part, preferred_element_type=jnp.float32
    ).astype(jnp.bfloat16)
    mixed_out = mixed_out.reshape(seq_count * frames_local, 1, item_count, heads_local * head_dim)
    attended = lax.all_to_all(mixed_out, "seq", split_axis=0, concat_axis=1, tiled=True)
    attended = attended.reshape(block_rows, heads_local * head_dim)
    branch_sum = lax.psum_scatter(
        jnp.dot(attended, w_out, preferred_element_type=jnp.float32).astype(jnp.bfloat16),
        ("head", "sub"),
        scatter_dimension=0,
        tiled=True,
    ).astype(jnp.float32)
    hidden = (frames_in.astype(jnp.float32) + branch_sum).astype(jnp.bfloat16)
    vit_own = normalize(hidden, vit_gain)
    vit_rows = lax.all_gather(vit_own, ("head", "sub"), axis=0, tiled=True)
    current = jnp.dot(vit_rows, w_pair[0], preferred_element_type=jnp.float32)
    ahead_proj = jnp.dot(vit_rows, w_pair[1], preferred_element_type=jnp.float32)
    ahead_proj = ahead_proj.reshape(frames_local, cols_local, -1)
    arrived = from_behind(ahead_proj[:1].astype(jnp.bfloat16), "seq", -frame_step).astype(
        jnp.float32
    )
    following = jnp.concatenate([ahead_proj[1:], arrived], axis=0).reshape(block_rows, -1)
    embedded = current + following
    activated = jax.nn.gelu(embedded, approximate=False).reshape(frames_local, cols_local, -1)
    seq_index = lax.axis_index("seq")
    first_token = seq_index * block_rows
    frame_first = first_token // total_cols
    col_first = first_token % total_cols
    patches = total_cols // ROLLS
    roll_ids = (col_first + jnp.arange(cols_local, dtype=jnp.int32)) // patches
    member = (roll_ids[None, :] == jnp.arange(ROLLS, dtype=jnp.int32)[:, None]).astype(
        jnp.float32
    ) / patches
    pooled = jnp.einsum("rp,fpe->fre", member, activated, precision=lax.Precision.HIGHEST)
    scored = jnp.einsum("fre,ea->fra", pooled, w_act, precision=lax.Precision.HIGHEST)
    frame_ids = frame_first + jnp.arange(frames_local, dtype=jnp.int32)
    selector = (pair_frames[:, :, None] == frame_ids[None, None, :]).astype(jnp.float32)
    partial_value = jnp.einsum("rjf,fra->rja", selector, scored, precision=lax.Precision.HIGHEST)
    actions = lax.psum(partial_value, ("seq", "head", "sub"))
    return (hidden, actions)


GRANT = pltpu.CompilerParams(vmem_limit_bytes=12 * 1024 * 1024)


def on_chip(value):
    return pltpu.with_memory_space_constraint(value, pltpu.VMEM)


def off_chip(value):
    return pltpu.with_memory_space_constraint(value, pltpu.HBM)


def swap(value, axis, mask):
    count = lax.axis_size(axis)
    pairs = [(source, source ^ mask) for source in range(count)]
    return on_chip(lax.ppermute(value, axis, pairs))


def lined(gain_ref):
    return jnp.concatenate([gain_ref[row : row + 1, :] for row in range(gain_ref.shape[0])], axis=1)


def scaled(rows, gain_row):
    mean_sq = jnp.mean(rows * rows, axis=-1, keepdims=True)
    return (rows * lax.rsqrt(mean_sq + EPS) * gain_row).astype(jnp.bfloat16)


def cut_kernel(seq_count, small, tokens_ref, *refs):
    small_refs, out_refs, sems = refs[:small], refs[small:-1], refs[-1]
    wide = out_refs[0].shape[0]
    place = lax.axis_index("seq")
    copies = []
    for step, out_ref in enumerate(out_refs[:seq_count]):
        first = pl.multiple_of((place ^ step) * wide, wide)
        source = tokens_ref.at[pl.ds(first, wide), :]
        copies.append(pltpu.make_async_copy(source, out_ref, sems.at[step]))
    for source, out_ref in zip(small_refs, out_refs[seq_count:]):
        copies.append(pltpu.make_async_copy(source, out_ref, sems.at[len(copies)]))
    for copy in copies:
        copy.start()
    for copy in copies:
        copy.wait()


def halve_kernel(cols, *refs):
    *piece_refs, mine_ref, pals_ref = refs
    for lower, (first_ref, second_ref) in enumerate(((pals_ref, mine_ref), (mine_ref, pals_ref))):

        @pl.when(lax.axis_index("sub") == 1 - lower)
        def _():
            for step, ref in enumerate(piece_refs):
                rows = slice(step * cols, (step + 1) * cols)
                first_ref[rows, :] = ref[:cols, :]
                second_ref[rows, :] = ref[cols:, :]


def attend_kernel(cols, heads, head_dim, *refs):
    *token_refs, gain_ref, wq_far, wq_pal, wo_far, wo_pal, out_ref = refs[:-5]
    normed_ref, mixed_ref, wq_own, wo_own, sems = refs[-5:]
    triple = 3 * head_dim
    inner = heads * head_dim
    group = 2 if heads % 2 == 0 else 1
    chunk = group * triple
    copies = []
    for first in range(0, heads * triple, chunk):
        piece = pl.ds(first, chunk)
        copies.append(
            pltpu.make_async_copy(wq_far.at[piece, :], wq_own.at[piece, :], sems.at[len(copies)])
        )
    copies.append(pltpu.make_async_copy(wo_far, wo_own, sems.at[len(copies)]))
    for copy in copies:
        copy.start()
    step = token_refs[0].shape[0]
    gain_row = lined(gain_ref)
    for place, ref in enumerate(token_refs):
        normed_ref[place * step : (place + 1) * step, :] = scaled(
            ref[...].astype(jnp.float32), gain_row
        )
    rows = normed_ref.shape[0]
    left = lax.broadcasted_iota(jnp.int32, (rows, rows), 0) % cols
    right = lax.broadcasted_iota(jnp.int32, (rows, rows), 1) % cols
    same = left == right
    for index, wq_ref in enumerate((wq_pal, wq_own)):
        for start in range(0, heads, group):
            if index == 1:
                copies[start // group].wait()
            qkv = lax.dot_general(
                wq_ref[start * triple : start * triple + chunk, :], normed_ref[...],
                (((1,), (1,)), ((), ())), preferred_element_type=jnp.float32,
            ).astype(jnp.bfloat16)
            for part in range(group):
                base = part * triple
                query = qkv[base : base + head_dim, :]
                key = qkv[base + head_dim : base + 2 * head_dim, :]
                val = qkv[base + 2 * head_dim : base + triple, :]
                scores = lax.dot_general(
                    key, query, (((0,), (0,)), ((), ())), preferred_element_type=jnp.float32
                ) * head_dim ** (-0.5)
                scores = jnp.where(same, scores, -jnp.inf)
                weights = jnp.exp(scores - jnp.max(scores, axis=0, keepdims=True))
                weights = weights * (1.0 / jnp.sum(weights, axis=0, keepdims=True))
                first = index * inner + (start + part) * head_dim
                mixed_ref[first : first + head_dim, :] = jnp.dot(
                    val, weights.astype(jnp.bfloat16), preferred_element_type=jnp.float32
                ).astype(jnp.bfloat16)
    total = None
    for index, wo_ref in enumerate((wo_pal, wo_own)):
        if index == 1:
            copies[-1].wait()
        product = lax.dot_general(
            mixed_ref[index * inner : (index + 1) * inner, :], wo_ref[...],
            (((0,), (0,)), ((), ())), preferred_element_type=jnp.float32,
        ).astype(jnp.bfloat16).astype(jnp.float32)
        total = product if total is None else total + product
    out_ref[...] = total.astype(jnp.bfloat16)


def pair_kernel(cols, frames, seq_count, split_count, patches, others, *refs):
    token_refs, refs = refs[:split_count], refs[split_count:]
    own_ref, refs = refs[0], refs[1:]
    other_refs, refs = refs[:others], refs[others:]
    gain_ref, wp_a, wp_b, wa_a, wa_b, pairs_ref, keep_ref, pass_ref, part_ref, *refs = refs
    hidden_ref, cur_ref, fol_ref = refs
    step = token_refs[0].shape[0]
    seq_place = lax.axis_index("seq")
    split_place = lax.axis_index(("head", "sub"))
    roll = (seq_place * 2 + lax.axis_index("sub")) * cols // patches
    for place, ref in enumerate(token_refs):
        rows = slice(place * step, (place + 1) * step)
        branch = own_ref[rows, :].astype(jnp.float32)
        for index, other in enumerate(other_refs):
            there = place ^ (2 * (index + 1))
            branch = branch + other[there * step : (there + 1) * step, :].astype(jnp.float32)
        hidden_ref[rows, :] = (ref[...].astype(jnp.float32) + branch).astype(jnp.bfloat16)
    keep_ref[...] = hidden_ref[:step, :]
    pass_ref[...] = hidden_ref[step : 2 * step, :]
    vit = scaled(hidden_ref[...].astype(jnp.float32), lined(gain_ref))
    scored = None
    for wp_ref, wa_ref in ((wp_a, wa_a), (wp_b, wa_b)):
        current = jnp.dot(vit, wp_ref[0], preferred_element_type=jnp.float32)
        ahead = jnp.dot(vit, wp_ref[1], preferred_element_type=jnp.float32)
        for split in range(split_count):
            for seq in range(seq_count):
                frame = (seq_place ^ seq) * split_count + (split_place ^ split)
                piece = slice((split * seq_count + seq) * cols, (split * seq_count + seq + 1) * cols)
                place = pl.ds(pl.multiple_of(frame * cols, cols), cols)
                cur_ref[place, :] = current[piece, :]
                fol_ref[place, :] = ahead[piece, :]
        embedded = cur_ref[: (frames - 1) * cols, :] + fol_ref[cols:, :]
        activated = 0.5 * embedded * (1.0 + lax.erf(embedded * (0.5**0.5)))
        pooled = jnp.sum(activated.reshape(frames - 1, cols, -1), axis=1) * (1.0 / patches)
        here = lax.dot_general(
            wa_ref[...], pooled, (((1,), (1,)), ((), ())),
            preferred_element_type=jnp.float32, precision=lax.Precision.HIGHEST,
        )
        scored = here if scored is None else scored + here
    wanted = pairs_ref.shape[1]
    part_ref[...] = jnp.zeros_like(part_ref)
    for index in range(ROLLS):
        chosen = pairs_ref[index : index + 1, :] == lax.broadcasted_iota(
            jnp.int32, (frames - 1, wanted), 0
        )
        first = index * LINES
        part_ref[first : first + scored.shape[0], :wanted] = jnp.dot(
            scored, jnp.where(chosen & (roll == index), 1.0, 0.0),
            preferred_element_type=jnp.float32, precision=lax.Precision.HIGHEST,
        )


def pack_kernel(cols, parts, kept_ref, arrived_ref, *refs):
    part_refs, block_refs = refs[:parts], refs[parts:]
    width = kept_ref.shape[1]
    total = part_refs[0][...]
    for ref in part_refs[1:]:
        total = total + ref[...]
    high = total.astype(jnp.bfloat16)
    low = (total - high.astype(jnp.float32)).astype(jnp.bfloat16)
    height, lanes = total.shape
    for block_ref in block_refs:
        block_ref[:height, width : width + lanes] = high
        block_ref[:height, width + lanes :] = low
    for lower, (first_ref, second_ref) in enumerate(
        ((arrived_ref, kept_ref), (kept_ref, arrived_ref))
    ):

        @pl.when(lax.axis_index("sub") == 1 - lower)
        def _():
            for step, block_ref in enumerate(block_refs):
                rows = slice(step * cols, (step + 1) * cols)
                block_ref[:cols, :width] = first_ref[rows, :]
                block_ref[cols:, :width] = second_ref[rows, :]


def place_kernel(seq_count, wide, *refs):
    block_refs, (hidden_ref, actions_ref) = refs[:seq_count], refs[seq_count:]
    width = hidden_ref.shape[1]
    lanes = (block_refs[0].shape[1] - width) // 2
    height = ROLLS * LINES
    total = None
    for step, ref in enumerate(block_refs):
        first = pl.multiple_of((lax.axis_index("seq") ^ step) * wide, wide)
        hidden_ref[pl.ds(first, wide), :] = ref[:, :width]
        part = ref[:height, width : width + lanes].astype(jnp.float32)
        part = part + ref[:height, width + lanes :].astype(jnp.float32)
        total = part if total is None else total + part
    outs, _, each = actions_ref.shape
    for roll in range(ROLLS):
        actions_ref[:, roll, :] = total[roll * LINES : roll * LINES + outs, :each]


def fast_shards(frames_in, attn_gain, w_qkv, w_out, vit_gain, w_pair, w_act, pair_frames):
    rows_own, width = frames_in.shape
    seq_count = lax.axis_size("seq")
    head_count = lax.axis_size("head")
    split_count = head_count * 2
    heads, triple = w_qkv.shape[1:]
    head_dim = triple // 3
    wide = rows_own // seq_count
    cols = wide // 2
    patches = rows_own // ROLLS
    vmem = pl.BlockSpec(memory_space=pltpu.VMEM)
    hbm = pl.BlockSpec(memory_space=pltpu.HBM)
    wq_own = jnp.transpose(w_qkv, (1, 2, 0)).reshape(heads * triple, width)
    wa_own = w_act.T
    small = [attn_gain.reshape(-1, 128), vit_gain.reshape(-1, 128), wa_own, pair_frames]
    cut = pl.pallas_call(
        functools.partial(cut_kernel, seq_count, len(small)),
        compiler_params=GRANT,
        in_specs=[hbm] * (1 + len(small)),
        out_specs=[vmem] * (seq_count + len(small)),
        out_shape=[pltpu.VMEM((wide, width), jnp.bfloat16)] * seq_count
        + [pltpu.VMEM(value.shape, value.dtype) for value in small],
        scratch_shapes=[pltpu.SemaphoreType.DMA((seq_count + len(small),))],
    )(off_chip(frames_in), *[off_chip(value) for value in small])
    pieces = cut[:seq_count]
    attn_gain, vit_gain, wa_own, pair_frames = cut[seq_count:]
    pieces = [pieces[0]] + [swap(pieces[step], "seq", step) for step in range(1, seq_count)]
    wq_pal = swap(wq_own, "sub", 1)
    wo_pal = swap(w_out, "sub", 1)
    wp_pal = swap(w_pair, "sub", 1)
    wa_pal = swap(wa_own, "sub", 1)
    half = pltpu.VMEM((seq_count * cols, width), jnp.bfloat16)
    mine, pals = pl.pallas_call(
        functools.partial(halve_kernel, cols),
        compiler_params=GRANT,
        in_specs=[vmem] * seq_count,
        out_specs=[vmem] * 2,
        out_shape=[half] * 2,
    )(*pieces)
    tokens = [mine] + [
        swap(pals if step & 1 else mine, ("head", "sub"), step)
        for step in range(1, split_count)
    ]
    rows = split_count * seq_count * cols
    inner = heads * head_dim
    branch = pl.pallas_call(
        functools.partial(attend_kernel, cols, heads, head_dim),
        compiler_params=GRANT,
        in_specs=[vmem] * (split_count + 1) + [hbm, vmem, hbm, vmem],
        out_specs=vmem,
        out_shape=pltpu.VMEM((rows, width), jnp.bfloat16),
        scratch_shapes=[
            pltpu.VMEM((rows, width), jnp.bfloat16),
            pltpu.VMEM((2 * inner, rows), jnp.bfloat16),
            pltpu.VMEM((3 * inner, width), jnp.bfloat16),
            pltpu.VMEM((inner, width), jnp.bfloat16),
            pltpu.SemaphoreType.DMA((heads + 1,)),
        ],
    )(*tokens, attn_gain, off_chip(wq_own), wq_pal, off_chip(w_out), wo_pal)
    others = [swap(branch, "head", step) for step in range(1, head_count)]
    embed = w_pair.shape[2]
    wanted = pair_frames.shape[1]
    kept, passed, part = pl.pallas_call(
        functools.partial(
            pair_kernel, cols, F, seq_count, split_count, patches, head_count - 1
        ),
        compiler_params=GRANT,
        in_specs=[vmem] * (split_count + head_count + 6),
        out_specs=[vmem] * 3,
        out_shape=(half, half, pltpu.VMEM((ROLLS * LINES, 128), jnp.float32)),
        scratch_shapes=[
            pltpu.VMEM((rows, width), jnp.bfloat16),
            pltpu.VMEM((rows, embed), jnp.float32),
            pltpu.VMEM((rows, embed), jnp.float32),
        ],
    )(
        *tokens, branch, *others, vit_gain, on_chip(w_pair), wp_pal,
        wa_own, wa_pal, pair_frames,
    )
    arrived = swap(passed, "sub", 1)
    parts = [part] + [swap(part, ("head", "sub"), step) for step in range(1, split_count)]
    blocks = pl.pallas_call(
        functools.partial(pack_kernel, cols, split_count),
        compiler_params=GRANT,
        in_specs=[vmem] * (2 + split_count),
        out_specs=[vmem] * seq_count,
        out_shape=[pltpu.VMEM((wide, width + 256), jnp.bfloat16)] * seq_count,
    )(kept, arrived, *parts)
    blocks = [blocks[0]] + [swap(blocks[step], "seq", step) for step in range(1, seq_count)]
    hidden, actions = pl.pallas_call(
        functools.partial(place_kernel, seq_count, wide),
        compiler_params=GRANT,
        in_specs=[vmem] * seq_count,
        out_shape=(
            jax.ShapeDtypeStruct((rows_own, width), jnp.bfloat16),
            jax.ShapeDtypeStruct((w_act.shape[1], ROLLS, wanted), jnp.float32),
        ),
    )(*blocks)
    return hidden, jnp.transpose(actions, (1, 2, 0))


def shards(frames_in, attn_gain, w_qkv, w_out, vit_gain, w_pair, w_act, pair_frames):
    seq_count = lax.axis_size("seq")
    head_count = lax.axis_size("head")
    rows_own = frames_in.shape[0]
    powers = all(count & (count - 1) == 0 for count in (seq_count, head_count))
    one_frame = seq_count * head_count * lax.axis_size("sub") == F
    tiled = rows_own % (seq_count * 16) == 0 and lax.axis_size("sub") == 2
    tiled = tiled and rows_own // seq_count >= ROLLS * LINES
    tiled = tiled and pair_frames.shape[1] <= 128 and w_act.shape[1] <= LINES
    tiled = tiled and frames_in.shape[1] % 128 == 0
    chosen = fast_shards if powers and one_frame and tiled else general_shards
    return chosen(frames_in, attn_gain, w_qkv, w_out, vit_gain, w_pair, w_act, pair_frames)


def solution(mesh):
    in_specs = (
        P(("groups", "seq", "head", "sub"), None),
        P(),
        P(None, ("head", "sub"), None),
        P(("head", "sub"), None),
        P(),
        P(None, None, ("head", "sub")),
        P(("head", "sub"), None),
        P("groups", None),
    )
    out_specs = (P(("groups", "seq", "head", "sub"), None), P("groups", None, None))
    return jax.shard_map(shards, mesh=mesh, in_specs=in_specs, out_specs=out_specs, check_vma=False)
```

profile of v0, /device:TPU:0, one launch (start us, length us, event | category | flops | bytes accessed | tf_op | source)
XLA Modules:
  0.0 59.3 jit_solution(11353819061877008200)
XLA Ops:
  0.6 0.6 collective-permute-start.6
  1.2 0.1 collective-permute-start.7
  1.3 0.4 collective-permute-start.9
  1.7 0.9 %shard_map.95 = (bf16[16,1536]{1,0:T(8,128)(2,1)S(1)}, bf16[16,1536]{1,0:T(8,128)(2,1)S(1)}, bf16[16,1536]{1,0:T(8,128)(2,1)S(1)}, bf16[16,1536]{1,0:T(8,128)(2,...) custom-call(bf16[64,1536]{1,0:T(8,128)(2,1)} %tokens_ref.1, ...), custom_call_target="tpu_custom_call" | custom-call | tf_op jit(solution)/shard_map/pallas_call | solution.py:326
  2.7 2.7 %collective-permute-start = (bf16[16,1536]{1,0:T(8,128)(2,1)S(1)}, bf16[16,1536]{1,0:T(8,128)(2,1)S(1)}, u32[]{:S(2)}, u32[]{:S(2)}) collective-permute-start(bf16[16,1536]{1,0:T(8,128)(2,1)S(1)} %get-tuple-element.22), channel_id=1, source_target_pairs={{0,4},{4,0},{8,12},{12,8},{1,5},{5,1},{9,13},{13,9},{2,6},{6,2},{1... | collective-permute-start | bytes 147464 | tf_op jit(solution)/shard_map/ppermute | solution.py:116
  5.4 2.6 %collective-permute-start.1 = (bf16[16,1536]{1,0:T(8,128)(2,1)S(1)}, bf16[16,1536]{1,0:T(8,128)(2,1)S(1)}, u32[]{:S(2)}, u32[]{:S(2)}) collective-permute-start(bf16[16,1536]{1,0:T(8,128)(2,1)S(1)} %get-tuple-element.23), channel_id=1, source_target_pairs={{0,8},{4,12},{8,0},{12,4},{1,9},{5,13},{9,1},{13,5},{2,10},{6,14},... | collective-permute-start | bytes 147464 | tf_op jit(solution)/shard_map/ppermute | solution.py:116
  7.9 0.0 collective-permute-done.refs_1_
  8.0 3.5 %collective-permute-start.2 = (bf16[16,1536]{1,0:T(8,128)(2,1)S(1)}, bf16[16,1536]{1,0:T(8,128)(2,1)S(1)}, u32[]{:S(2)}, u32[]{:S(2)}) collective-permute-start(bf16[16,1536]{1,0:T(8,128)(2,1)S(1)} %get-tuple-element.24), channel_id=1, source_target_pairs={{0,12},{4,8},{8,4},{12,0},{1,13},{5,9},{9,5},{13,1},{2,14},{6,10},... | collective-permute-start | bytes 147464 | tf_op jit(solution)/shard_map/ppermute | solution.py:116
  11.5 0.0 collective-permute-done.1.refs_2_
  11.5 2.4 %collective-permute-done.2.refs_3_ = bf16[16,1536]{1,0:T(8,128)(2,1)S(1)} collective-permute-done((bf16[16,1536]{1,0:T(8,128)(2,1)S(1)}, bf16[16,1536]{1,0:T(8,128)(2,1)S(1)}, u32[]{:S(2)}, u32[]{:S(2)}) %collective-permute-start.2) | collective-permute-done | bytes 49184 | tf_op jit(solution)/shard_map/ppermute | solution.py:116
  13.9 1.6 %collective-permute-start.4 = (bf16[32,1536]{1,0:T(8,128)(2,1)S(1)}, bf16[32,1536]{1,0:T(8,128)(2,1)S(1)}, u32[]{:S(2)}, u32[]{:S(2)}) collective-permute-start(bf16[32,1536]{1,0:T(8,128)(2,1)S(1)} %get-tuple-element.25.refs_0_), channel_id=1, source_target_pairs={{0,2},{1,3},{2,0},{3,1},{4,6},{5,7},{6,4},{7,5},{8,10},{9,11},{10,... | collective-permute-start | bytes 294920 | tf_op jit(solution)/shard_map/ppermute | solution.py:116
  15.4 0.0 collective-permute-start.3
  15.4 3.1 %collective-permute-done.4.refs_2_ = bf16[32,1536]{1,0:T(8,128)(2,1)S(1)} collective-permute-done((bf16[32,1536]{1,0:T(8,128)(2,1)S(1)}, bf16[32,1536]{1,0:T(8,128)(2,1)S(1)}, u32[]{:S(2)}, u32[]{:S(2)}) %collective-permute-start.4) | collective-permute-done | bytes 98336 | tf_op jit(solution)/shard_map/ppermute | solution.py:116
  18.5 0.0 collective-permute-start.5
  18.5 0.0 collective-permute-done.3.refs_1_
  18.5 5.0 %collective-permute-done.5.refs_3_ = bf16[32,1536]{1,0:T(8,128)(2,1)S(1)} collective-permute-done((bf16[32,1536]{1,0:T(8,128)(2,1)S(1)}, bf16[32,1536]{1,0:T(8,128)(2,1)S(1)}, u32[]{:S(2)}, u32[]{:S(2)}) %collective-permute-start.5) | collective-permute-done | bytes 98336 | tf_op jit(solution)/shard_map/ppermute | solution.py:116
  23.6 0.0 collective-permute-done.7.refs_8_
  23.6 0.0 collective-permute-done.6.refs_6_
  23.6 0.0 copy-start
  23.6 8.2 %shard_map.97.refs_4_ = bf16[128,1536]{1,0:T(8,128)(2,1)S(1)} custom-call(bf16[32,1536]{1,0:T(8,128)(2,1)S(1)} %get-tuple-element.25.refs_0_, bf16[32,1536]{1,0:T(8,128)(2,1)S(1)} %collective-permute-done.3.refs_1_, bf16[32,1536]{1,0:T(8,128)(2,1)S(1)} %collective-permute-done.4.refs_2_, bf16[32,1536]{1,0:T(8,128)(2,1)S(1)} %collective-permute-done.5.refs_3_, ...), custom_call_target="tpu_custom_call" | custom-call | tf_op jit(solution)/shard_map/pallas_call | solution.py:356
  31.8 0.7 %collective-permute-start.8 = (bf16[128,1536]{1,0:T(8,128)(2,1)S(1)}, bf16[128,1536]{1,0:T(8,128)(2,1)S(1)}, u32[]{:S(2)}, u32[]{:S(2)}) collective-permute-start(bf16[128,1536]{1,0:T(8,128)(2,1)S(1)} %shard_map.97.refs_4_), channel_id=1, source_target_pairs={{0,2},{2,0},{1,3},{3,1},{4,6},{6,4},{5,7},{7,5},{8,10},{10,8},{9,1... | collective-permute-start | bytes 1179656 | tf_op jit(solution)/shard_map/ppermute | solution.py:116
  32.5 0.0 collective-permute-start.10
  32.5 1.2 %collective-permute-done.10.refs_10_ = f32[7,256]{1,0:T(8,128)S(1)} collective-permute-done((f32[7,256]{1,0:T(8,128)S(1)}, f32[7,256]{1,0:T(8,128)S(1)}, u32[]{:S(2)}, u32[]{:S(2)}) %collective-permute-start.10) | collective-permute-done | bytes 7200 | tf_op jit(solution)/shard_map/ppermute | solution.py:116
  33.7 0.0 collective-permute-done.9.refs_8_
  33.7 9.3 %collective-permute-done.8.refs_5_ = bf16[128,1536]{1,0:T(8,128)(2,1)S(1)} collective-permute-done((bf16[128,1536]{1,0:T(8,128)(2,1)S(1)}, bf16[128,1536]{1,0:T(8,128)(2,1)S(1)}, u32[]{:S(2)}, u32[]{:S(2)}) %collective-permute-start.8) | collective-permute-done | bytes 393248 | tf_op jit(solution)/shard_map/ppermute | solution.py:116
  43.0 0.0 copy-done
  43.0 1.2 %shard_map.98 = (bf16[32,1536]{1,0:T(8,128)(2,1)S(1)}, bf16[32,1536]{1,0:T(8,128)(2,1)S(1)}, f32[16,128]{1,0:T(8,128)S(1)}) custom-call(bf16[32,1536]{1,0:T(8,128)(2,1)S(1)} %get-tuple-element.25.refs_0_, bf16[32,1536]{1,0:T(8,128)(2,1)S(1)} %collective-permute-done.3.refs_1_, bf16[32,1536]{1,0:T(8,128)(2,1)S(1)} %collective-permute-done.4.refs_2_, ...), custom_call_target="tpu_custom_call" | custom-call | tf_op jit(solution)/shard_map/pallas_call | solution.py:373
  44.3 0.0 collective-permute-start.11
  44.3 0.5 collective-permute-start.12
  44.8 0.3 collective-permute-start.13
  45.1 1.1 %collective-permute-start.14 = (f32[16,128]{1,0:T(8,128)S(1)}, f32[16,128]{1,0:T(8,128)S(1)}, u32[]{:S(2)}, u32[]{:S(2)}) collective-permute-start(f32[16,128]{1,0:T(8,128)S(1)} %get-tuple-element.33.refs_0_), channel_id=1, source_target_pairs={{0,3},{1,2},{2,1},{3,0},{4,7},{5,6},{6,5},{7,4},{8,11},{9,10},{10,... | collective-permute-start | bytes 24584 | tf_op jit(solution)/shard_map/ppermute | solution.py:116
  46.2 0.0 collective-permute-done.12.refs_1_
  46.2 2.3 %collective-permute-done.13.refs_2_ = f32[16,128]{1,0:T(8,128)S(1)} collective-permute-done((f32[16,128]{1,0:T(8,128)S(1)}, f32[16,128]{1,0:T(8,128)S(1)}, u32[]{:S(2)}, u32[]{:S(2)}) %collective-permute-start.13) | collective-permute-done | bytes 8224 | tf_op jit(solution)/shard_map/ppermute | solution.py:116
  48.4 0.0 collective-permute-done.14.refs_3_
  48.4 0.0 collective-permute-done.11.arrived_ref
  48.5 0.1 collective-permute-start.15
  48.6 4.1 %collective-permute-start.16 = (bf16[16,1792]{1,0:T(8,128)(2,1)S(1)}, bf16[16,1792]{1,0:T(8,128)(2,1)S(1)}, u32[]{:S(2)}, u32[]{:S(2)}) collective-permute-start(bf16[16,1792]{1,0:T(8,128)(2,1)S(1)} %get-tuple-element.36), channel_id=1, source_target_pairs={{0,8},{4,12},{8,0},{12,4},{1,9},{5,13},{9,1},{13,5},{2,10},{6,14},... | collective-permute-start | bytes 172040 | tf_op jit(solution)/shard_map/ppermute | solution.py:116
  52.6 0.3 collective-permute-start.17
  52.9 0.0 collective-permute-done.15.refs_1_
  52.9 3.2 %collective-permute-done.16.refs_2_ = bf16[16,1792]{1,0:T(8,128)(2,1)S(1)} collective-permute-done((bf16[16,1792]{1,0:T(8,128)(2,1)S(1)}, bf16[16,1792]{1,0:T(8,128)(2,1)S(1)}, u32[]{:S(2)}, u32[]{:S(2)}) %collective-permute-start.16) | collective-permute-done | bytes 57376 | tf_op jit(solution)/shard_map/ppermute | solution.py:116
  56.2 2.4 %collective-permute-done.17.refs_3_ = bf16[16,1792]{1,0:T(8,128)(2,1)S(1)} collective-permute-done((bf16[16,1792]{1,0:T(8,128)(2,1)S(1)}, bf16[16,1792]{1,0:T(8,128)(2,1)S(1)}, u32[]{:S(2)}, u32[]{:S(2)}) %collective-permute-start.17) | collective-permute-done | bytes 57376 | tf_op jit(solution)/shard_map/ppermute | solution.py:116
  58.6 0.7 %shard_map.100 = (bf16[64,1536]{1,0:T(8,128)(2,1)}, f32[7,2,15]{2,1,0:T(2,128)}) custom-call(bf16[16,1792]{1,0:T(8,128)(2,1)S(1)} %get-tuple-element.34.refs_0_, bf16[16,1792]{1,0:T(8,128)(2,1)S(1)} %collective-permute-done.15.refs_1_, bf16[16,1792]{1,0:T(8,128)(2,1)S(1)} %collective-permute-done.16.refs_2_, bf16[16,1792]{1,0:T(8,128)(2,1)S(1)} %collective-permute-done.17.refs_3_), custom_call_target="tpu_custom_call" | custom-call | tf_op jit(solution)/shard_map/pallas_call | solution.py:400
  (2 shorter events, 0.0 us)
Async XLA Ops:
  0.6 23.0 %collective-permute-start.6 = (bf16[1152,1536]{1,0:T(8,128)(2,1)}, bf16[1152,1536]{1,0:T(8,128)(2,1)S(1)}, u32[]{:S(2)}, u32[]{:S(2)}) collective-permute-start(bf16[1152,1536]{1,0:T(8,128)(2,1)} %bitcast.7), channel_id=1, source_target_pairs={{0,1},{1,0},{2,3},{3,2},{4,5},{5,4},{6,7},{7,6},{8,9},{9,8},{10,11... | collective-permute-start | bytes 10616840 | tf_op jit(solution)/shard_map/ppermute | solution.py:116
  1.2 22.4 %collective-permute-start.7 = (bf16[384,1536]{1,0:T(8,128)(2,1)}, bf16[384,1536]{1,0:T(8,128)(2,1)S(1)}, u32[]{:S(2)}, u32[]{:S(2)}) collective-permute-start(bf16[384,1536]{1,0:T(8,128)(2,1)} %refs_7_.2), channel_id=1, source_target_pairs={{0,1},{1,0},{2,3},{3,2},{4,5},{5,4},{6,7},{7,6},{8,9},{9,8},{10,11... | collective-permute-start | bytes 3538952 | tf_op jit(solution)/shard_map/ppermute | solution.py:116
  1.3 32.4 %collective-permute-start.9 = (bf16[2,1536,256]{2,1,0:T(8,128)(2,1)}, bf16[2,1536,256]{2,1,0:T(8,128)(2,1)S(1)}, u32[]{:S(2)}, u32[]{:S(2)}) collective-permute-start(bf16[2,1536,256]{2,1,0:T(8,128)(2,1)} %refs_7_.3), channel_id=1, source_target_pairs={{0,1},{1,0},{2,3},{3,2},{4,5},{5,4},{6,7},{7,6},{8,9},{9,8},{10,11... | collective-permute-start | bytes 4718600 | tf_op jit(solution)/shard_map/ppermute | solution.py:116
  2.7 5.3 %collective-permute-start = (bf16[16,1536]{1,0:T(8,128)(2,1)S(1)}, bf16[16,1536]{1,0:T(8,128)(2,1)S(1)}, u32[]{:S(2)}, u32[]{:S(2)}) collective-permute-start(bf16[16,1536]{1,0:T(8,128)(2,1)S(1)} %get-tuple-element.22), channel_id=1, source_target_pairs={{0,4},{4,0},{8,12},{12,8},{1,5},{5,1},{9,13},{13,9},{2,6},{6,2},{1... | collective-permute-start | bytes 147464 | tf_op jit(solution)/shard_map/ppermute | solution.py:116
  5.4 6.1 %collective-permute-start.1 = (bf16[16,1536]{1,0:T(8,128)(2,1)S(1)}, bf16[16,1536]{1,0:T(8,128)(2,1)S(1)}, u32[]{:S(2)}, u32[]{:S(2)}) collective-permute-start(bf16[16,1536]{1,0:T(8,128)(2,1)S(1)} %get-tuple-element.23), channel_id=1, source_target_pairs={{0,8},{4,12},{8,0},{12,4},{1,9},{5,13},{9,1},{13,5},{2,10},{6,14},... | collective-permute-start | bytes 147464 | tf_op jit(solution)/shard_map/ppermute | solution.py:116
  8.0 5.9 %collective-permute-start.2 = (bf16[16,1536]{1,0:T(8,128)(2,1)S(1)}, bf16[16,1536]{1,0:T(8,128)(2,1)S(1)}, u32[]{:S(2)}, u32[]{:S(2)}) collective-permute-start(bf16[16,1536]{1,0:T(8,128)(2,1)S(1)} %get-tuple-element.24), channel_id=1, source_target_pairs={{0,12},{4,8},{8,4},{12,0},{1,13},{5,9},{9,5},{13,1},{2,14},{6,10},... | collective-permute-start | bytes 147464 | tf_op jit(solution)/shard_map/ppermute | solution.py:116
  13.9 4.7 %collective-permute-start.4 = (bf16[32,1536]{1,0:T(8,128)(2,1)S(1)}, bf16[32,1536]{1,0:T(8,128)(2,1)S(1)}, u32[]{:S(2)}, u32[]{:S(2)}) collective-permute-start(bf16[32,1536]{1,0:T(8,128)(2,1)S(1)} %get-tuple-element.25.refs_0_), channel_id=1, source_target_pairs={{0,2},{1,3},{2,0},{3,1},{4,6},{5,7},{6,4},{7,5},{8,10},{9,11},{10,... | collective-permute-start | bytes 294920 | tf_op jit(solution)/shard_map/ppermute | solution.py:116
  15.4 3.1 %collective-permute-start.3 = (bf16[32,1536]{1,0:T(8,128)(2,1)S(1)}, bf16[32,1536]{1,0:T(8,128)(2,1)S(1)}, u32[]{:S(2)}, u32[]{:S(2)}) collective-permute-start(bf16[32,1536]{1,0:T(8,128)(2,1)S(1)} %get-tuple-element.26), channel_id=1, source_target_pairs={{0,1},{1,0},{2,3},{3,2},{4,5},{5,4},{6,7},{7,6},{8,9},{9,8},{10,11... | collective-permute-start | bytes 294920 | tf_op jit(solution)/shard_map/ppermute | solution.py:116
  18.5 5.1 %collective-permute-start.5 = (bf16[32,1536]{1,0:T(8,128)(2,1)S(1)}, bf16[32,1536]{1,0:T(8,128)(2,1)S(1)}, u32[]{:S(2)}, u32[]{:S(2)}) collective-permute-start(bf16[32,1536]{1,0:T(8,128)(2,1)S(1)} %get-tuple-element.26), channel_id=1, source_target_pairs={{0,3},{1,2},{2,1},{3,0},{4,7},{5,6},{6,5},{7,4},{8,11},{9,10},{10,... | collective-permute-start | bytes 294920 | tf_op jit(solution)/shard_map/ppermute | solution.py:116
  23.6 19.4 %copy-start = (bf16[2,1536,256]{2,1,0:T(8,128)(2,1)S(1)}, bf16[2,1536,256]{2,1,0:T(8,128)(2,1)}, u32[]{:S(2)}) copy-start(bf16[2,1536,256]{2,1,0:T(8,128)(2,1)} %refs_7_.3) | copy-start | bytes 4718596
  31.8 11.2 %collective-permute-start.8 = (bf16[128,1536]{1,0:T(8,128)(2,1)S(1)}, bf16[128,1536]{1,0:T(8,128)(2,1)S(1)}, u32[]{:S(2)}, u32[]{:S(2)}) collective-permute-start(bf16[128,1536]{1,0:T(8,128)(2,1)S(1)} %shard_map.97.refs_4_), channel_id=1, source_target_pairs={{0,2},{2,0},{1,3},{3,1},{4,6},{6,4},{5,7},{7,5},{8,10},{10,8},{9,1... | collective-permute-start | bytes 1179656 | tf_op jit(solution)/shard_map/ppermute | solution.py:116
  32.5 1.2 %collective-permute-start.10 = (f32[7,256]{1,0:T(8,128)S(1)}, f32[7,256]{1,0:T(8,128)S(1)}, u32[]{:S(2)}, u32[]{:S(2)}) collective-permute-start(f32[7,256]{1,0:T(8,128)S(1)} %get-tuple-element.29.refs_9_), channel_id=1, source_target_pairs={{0,1},{1,0},{2,3},{3,2},{4,5},{5,4},{6,7},{7,6},{8,9},{9,8},{10,11... | collective-permute-start | bytes 21512 | tf_op jit(solution)/shard_map/ppermute | solution.py:116
  44.3 4.2 %collective-permute-start.11 = (bf16[32,1536]{1,0:T(8,128)(2,1)S(1)}, bf16[32,1536]{1,0:T(8,128)(2,1)S(1)}, u32[]{:S(2)}, u32[]{:S(2)}) collective-permute-start(bf16[32,1536]{1,0:T(8,128)(2,1)S(1)} %get-tuple-element.32), channel_id=1, source_target_pairs={{0,1},{1,0},{2,3},{3,2},{4,5},{5,4},{6,7},{7,6},{8,9},{9,8},{10,11... | collective-permute-start | bytes 294920 | tf_op jit(solution)/shard_map/ppermute | solution.py:116
  44.3 1.9 %collective-permute-start.12 = (f32[16,128]{1,0:T(8,128)S(1)}, f32[16,128]{1,0:T(8,128)S(1)}, u32[]{:S(2)}, u32[]{:S(2)}) collective-permute-start(f32[16,128]{1,0:T(8,128)S(1)} %get-tuple-element.33.refs_0_), channel_id=1, source_target_pairs={{0,1},{1,0},{2,3},{3,2},{4,5},{5,4},{6,7},{7,6},{8,9},{9,8},{10,11... | collective-permute-start | bytes 24584 | tf_op jit(solution)/shard_map/ppermute | solution.py:116
  44.8 3.7 %collective-permute-start.13 = (f32[16,128]{1,0:T(8,128)S(1)}, f32[16,128]{1,0:T(8,128)S(1)}, u32[]{:S(2)}, u32[]{:S(2)}) collective-permute-start(f32[16,128]{1,0:T(8,128)S(1)} %get-tuple-element.33.refs_0_), channel_id=1, source_target_pairs={{0,2},{1,3},{2,0},{3,1},{4,6},{5,7},{6,4},{7,5},{8,10},{9,11},{10,... | collective-permute-start | bytes 24584 | tf_op jit(solution)/shard_map/ppermute | solution.py:116
  45.1 3.4 %collective-permute-start.14 = (f32[16,128]{1,0:T(8,128)S(1)}, f32[16,128]{1,0:T(8,128)S(1)}, u32[]{:S(2)}, u32[]{:S(2)}) collective-permute-start(f32[16,128]{1,0:T(8,128)S(1)} %get-tuple-element.33.refs_0_), channel_id=1, source_target_pairs={{0,3},{1,2},{2,1},{3,0},{4,7},{5,6},{6,5},{7,4},{8,11},{9,10},{10,... | collective-permute-start | bytes 24584 | tf_op jit(solution)/shard_map/ppermute | solution.py:116
  48.5 4.5 %collective-permute-start.15 = (bf16[16,1792]{1,0:T(8,128)(2,1)S(1)}, bf16[16,1792]{1,0:T(8,128)(2,1)S(1)}, u32[]{:S(2)}, u32[]{:S(2)}) collective-permute-start(bf16[16,1792]{1,0:T(8,128)(2,1)S(1)} %get-tuple-element.35), channel_id=1, source_target_pairs={{0,4},{4,0},{8,12},{12,8},{1,5},{5,1},{9,13},{13,9},{2,6},{6,2},{1... | collective-permute-start | bytes 172040 | tf_op jit(solution)/shard_map/ppermute | solution.py:116
  48.6 7.6 %collective-permute-start.16 = (bf16[16,1792]{1,0:T(8,128)(2,1)S(1)}, bf16[16,1792]{1,0:T(8,128)(2,1)S(1)}, u32[]{:S(2)}, u32[]{:S(2)}) collective-permute-start(bf16[16,1792]{1,0:T(8,128)(2,1)S(1)} %get-tuple-element.36), channel_id=1, source_target_pairs={{0,8},{4,12},{8,0},{12,4},{1,9},{5,13},{9,1},{13,5},{2,10},{6,14},... | collective-permute-start | bytes 172040 | tf_op jit(solution)/shard_map/ppermute | solution.py:116
  52.6 6.0 %collective-permute-start.17 = (bf16[16,1792]{1,0:T(8,128)(2,1)S(1)}, bf16[16,1792]{1,0:T(8,128)(2,1)S(1)}, u32[]{:S(2)}, u32[]{:S(2)}) collective-permute-start(bf16[16,1792]{1,0:T(8,128)(2,1)S(1)} %get-tuple-element.37), channel_id=1, source_target_pairs={{0,12},{4,8},{8,4},{12,0},{1,13},{5,9},{9,5},{13,1},{2,14},{6,10},... | collective-permute-start | bytes 172040 | tf_op jit(solution)/shard_map/ppermute | solution.py:116
where the time goes:
time: 59.5 us; the launch traced here: 59.3 us
  waiting for transfers between devices  29 us (49%)
  starting transfers between devices  18.5 us (31%)
  Pallas kernels  11.1 us (19%)
  between operations  0.69 us (1%)
    ppermute x18, waiting for transfers between devices, swap(): return on_chip(lax.ppermute(value, axis, pairs))  29 us
    ppermute x18, starting transfers between devices, swap(): return on_chip(lax.ppermute(value, axis, pairs))  18.5 us
    pallas_call x1, Pallas kernels, fast_shards(): pl.pallas_call(functools.partial(attend_kernel, cols, heads, head_dim), c...  8.22 us
    pallas_call x1, Pallas kernels, fast_shards(): pl.pallas_call(functools.partial(pair_kernel, cols, F, seq_count, split_c...  1.23 us
  transfers between devices with their start and end apart: 18, of which 8 were waited for; matrix products, arithmetic and copies ran while one was open for 0% of the time, Pallas kernels for 15%

commit v1 on v0

--- a/solution.py
+++ b/solution.py
@@ -154,22 +154,30 @@
                 second_ref[rows, :] = ref[cols:, :]
 
 
+def aligned(value, step):
+    return value if isinstance(value, int) else pl.multiple_of(value, step)
+
+
+def each(count, body):
+    lax.fori_loop(0, count, lambda index, carry: (body(index), carry)[1], 0)
+
+
 def attend_kernel(cols, heads, head_dim, *refs):
-    *token_refs, gain_ref, wq_far, wq_pal, wo_far, wo_pal, out_ref = refs[:-5]
-    normed_ref, mixed_ref, wq_own, wo_own, sems = refs[-5:]
+    *token_refs, gain_ref, wq_far, wq_pal, wo_far, wo_pal, out_ref = refs[:-6]
+    normed_ref, qkv_ref, mixed_ref, wq_own, wo_own, sems = refs[-6:]
     triple = 3 * head_dim
     inner = heads * head_dim
     group = 2 if heads % 2 == 0 else 1
     chunk = group * triple
-    copies = []
-    for first in range(0, heads * triple, chunk):
-        piece = pl.ds(first, chunk)
-        copies.append(
-            pltpu.make_async_copy(wq_far.at[piece, :], wq_own.at[piece, :], sems.at[len(copies)])
-        )
-    copies.append(pltpu.make_async_copy(wo_far, wo_own, sems.at[len(copies)]))
-    for copy in copies:
-        copy.start()
+
+    def fetch(index):
+        piece = pl.ds(aligned(index * chunk, chunk), chunk)
+        return pltpu.make_async_copy(wq_far.at[piece, :], wq_own.at[piece, :], sems.at[index])
+
+    for index in range(heads // group):
+        fetch(index).start()
+    fetch_out = pltpu.make_async_copy(wo_far, wo_own, sems.at[heads // group])
+    fetch_out.start()
     step = token_refs[0].shape[0]
     gain_row = lined(gain_ref)
     for place, ref in enumerate(token_refs):
@@ -177,36 +185,44 @@
             ref[...].astype(jnp.float32), gain_row
         )
     rows = normed_ref.shape[0]
+
+    def project(wq_ref, source, size, target):
+        qkv_ref[pl.ds(aligned(target, head_dim), size), :] = lax.dot_general(
+            wq_ref[pl.ds(aligned(source, size), size), :], normed_ref[...],
+            (((1,), (1,)), ((), ())), preferred_element_type=jnp.float32,
+        ).astype(jnp.bfloat16)
+
+    large = heads * triple // group
+
+    def project_pal(index):
+        project(wq_pal, index * large, large, index * large)
+
+    def project_own(index):
+        fetch(index).wait()
+        project(wq_own, index * chunk, chunk, heads * triple + index * chunk)
+
+    each(group, project_pal)
+    each(heads // group, project_own)
     left = lax.broadcasted_iota(jnp.int32, (rows, rows), 0) % cols
     right = lax.broadcasted_iota(jnp.int32, (rows, rows), 1) % cols
     same = left == right
-    for index, wq_ref in enumerate((wq_pal, wq_own)):
-        for start in range(0, heads, group):
-            if index == 1:
-                copies[start // group].wait()
-            qkv = lax.dot_general(
-                wq_ref[start * triple : start * triple + chunk, :], normed_ref[...],
-                (((1,), (1,)), ((), ())), preferred_element_type=jnp.float32,
-            ).astype(jnp.bfloat16)
-            for part in range(group):
-                base = part * triple
-                query = qkv[base : base + head_dim, :]
-                key = qkv[base + head_dim : base + 2 * head_dim, :]
-                val = qkv[base + 2 * head_dim : base + triple, :]
-                scores = lax.dot_general(
-                    key, query, (((0,), (0,)), ((), ())), preferred_element_type=jnp.float32
-                ) * head_dim ** (-0.5)
-                scores = jnp.where(same, scores, -jnp.inf)
-                weights = jnp.exp(scores - jnp.max(scores, axis=0, keepdims=True))
-                weights = weights * (1.0 / jnp.sum(weights, axis=0, keepdims=True))
-                first = index * inner + (start + part) * head_dim
-                mixed_ref[first : first + head_dim, :] = jnp.dot(
-                    val, weights.astype(jnp.bfloat16), preferred_element_type=jnp.float32
-                ).astype(jnp.bfloat16)
+    for head in range(2 * heads):
+        base = head * triple
+        query = qkv_ref[base : base + head_dim, :]
+        key = qkv_ref[base + head_dim : base + 2 * head_dim, :]
+        val = qkv_ref[base + 2 * head_dim : base + triple, :]
+        scores = lax.dot_general(
+            key, query, (((0,), (0,)), ((), ())), preferred_element_type=jnp.float32
+        ) * head_dim ** (-0.5)
+        scores = jnp.where(same, scores, -jnp.inf)
+        weights = jnp.exp(scores - jnp.max(scores, axis=0, keepdims=True))
+        weights = weights * (1.0 / jnp.sum(weights, axis=0, keepdims=True))
+        mixed_ref[head * head_dim : (head + 1) * head_dim, :] = jnp.dot(
+            val, weights.astype(jnp.bfloat16), preferred_element_type=jnp.float32
+        ).astype(jnp.bfloat16)
+    fetch_out.wait()
     total = None
     for index, wo_ref in enumerate((wo_pal, wo_own)):
-        if index == 1:
-            copies[-1].wait()
         product = lax.dot_general(
             mixed_ref[index * inner : (index + 1) * inner, :], wo_ref[...],
             (((0,), (0,)), ((), ())), preferred_element_type=jnp.float32,
@@ -361,6 +377,7 @@
         out_shape=pltpu.VMEM((rows, width), jnp.bfloat16),
         scratch_shapes=[
             pltpu.VMEM((rows, width), jnp.bfloat16),
+            pltpu.VMEM((6 * inner, rows), jnp.bfloat16),
             pltpu.VMEM((2 * inner, rows), jnp.bfloat16),
             pltpu.VMEM((3 * inner, width), jnp.bfloat16),
             pltpu.VMEM((inner, width), jnp.bfloat16),

time: 59.5 us -> 55.4 us (0.931)
  Pallas kernels: 11.1 us -> 7.05 us
    pallas_call x1, Pallas kernels: 8.22 us -> 4.14 us  [fast_shards(): pl.pallas_call(functools.partial(attend_kernel, cols, heads, head_dim), c...]
  transfers between devices with their start and end apart: 18 -> 18, of which waited for: 8 -> 8; matrix products, arithmetic and copies ran while one was open for 0% -> 0% of each run, Pallas kernels for 15% -> 9%
where the time goes in v1:
time: 55.4 us; the launch traced here: 55.2 us
  waiting for transfers between devices  29 us (52%)
  starting transfers between devices  18.5 us (33%)
  Pallas kernels  7.05 us (13%)
  between operations  0.69 us (1%)
    ppermute x18, waiting for transfers between devices, swap(): return on_chip(lax.ppermute(value, axis, pairs))  29 us
    ppermute x18, starting transfers between devices, swap(): return on_chip(lax.ppermute(value, axis, pairs))  18.5 us
    pallas_call x1, Pallas kernels, fast_shards(): pl.pallas_call(functools.partial(attend_kernel, cols, heads, head_dim), c...  4.14 us
    pallas_call x1, Pallas kernels, fast_shards(): pl.pallas_call(functools.partial(pair_kernel, cols, F, seq_count, split_c...  1.23 us
  transfers between devices with their start and end apart: 18, of which 8 were waited for; matrix products, arithmetic and copies ran while one was open for 0% of the time, Pallas kernels for 9%

profile of v1, /device:TPU:0, one launch (start us, length us, event | category | flops | bytes accessed | tf_op | source)
XLA Modules:
  0.0 55.2 jit_solution(16191615512730401243)
XLA Ops:
  0.6 0.6 %collective-permute-start.6 = (bf16[1152,1536]{1,0:T(8,128)(2,1)}, bf16[1152,1536]{1,0:T(8,128)(2,1)S(1)}, u32[]{:S(2)}, u32[]{:S(2)}) collective-permute-start(bf16[1152,1536]{1,0:T(8,128)(2,1)} %bitcast.7), channel_id=1, source_target_pairs={{0,1},{1,0},{2,3},{3,2},{4,5},{5,4},{6,7},{7,6},{8,9},{9,8},{10,11... | collective-permute-start | bytes 10616840 | tf_op jit(solution)/shard_map/ppermute | solution.py:116
  1.2 0.1 collective-permute-start.7
  1.3 0.4 collective-permute-start.9
  1.7 0.9 %shard_map.95 = (bf16[16,1536]{1,0:T(8,128)(2,1)S(1)}, bf16[16,1536]{1,0:T(8,128)(2,1)S(1)}, bf16[16,1536]{1,0:T(8,128)(2,1)S(1)}, bf16[16,1536]{1,0:T(8,128)(2,...) custom-call(bf16[64,1536]{1,0:T(8,128)(2,1)} %tokens_ref.1, ...), custom_call_target="tpu_custom_call" | custom-call | tf_op jit(solution)/shard_map/pallas_call | solution.py:342
  2.7 2.7 %collective-permute-start = (bf16[16,1536]{1,0:T(8,128)(2,1)S(1)}, bf16[16,1536]{1,0:T(8,128)(2,1)S(1)}, u32[]{:S(2)}, u32[]{:S(2)}) collective-permute-start(bf16[16,1536]{1,0:T(8,128)(2,1)S(1)} %get-tuple-element.22), channel_id=1, source_target_pairs={{0,4},{4,0},{8,12},{12,8},{1,5},{5,1},{9,13},{13,9},{2,6},{6,2},{1... | collective-permute-start | bytes 147464 | tf_op jit(solution)/shard_map/ppermute | solution.py:116
  5.4 2.6 %collective-permute-start.1 = (bf16[16,1536]{1,0:T(8,128)(2,1)S(1)}, bf16[16,1536]{1,0:T(8,128)(2,1)S(1)}, u32[]{:S(2)}, u32[]{:S(2)}) collective-permute-start(bf16[16,1536]{1,0:T(8,128)(2,1)S(1)} %get-tuple-element.23), channel_id=1, source_target_pairs={{0,8},{4,12},{8,0},{12,4},{1,9},{5,13},{9,1},{13,5},{2,10},{6,14},... | collective-permute-start | bytes 147464 | tf_op jit(solution)/shard_map/ppermute | solution.py:116
  7.9 0.0 collective-permute-done.refs_1_
  8.0 3.5 %collective-permute-start.2 = (bf16[16,1536]{1,0:T(8,128)(2,1)S(1)}, bf16[16,1536]{1,0:T(8,128)(2,1)S(1)}, u32[]{:S(2)}, u32[]{:S(2)}) collective-permute-start(bf16[16,1536]{1,0:T(8,128)(2,1)S(1)} %get-tuple-element.24), channel_id=1, source_target_pairs={{0,12},{4,8},{8,4},{12,0},{1,13},{5,9},{9,5},{13,1},{2,14},{6,10},... | collective-permute-start | bytes 147464 | tf_op jit(solution)/shard_map/ppermute | solution.py:116
  11.5 0.0 collective-permute-done.1.refs_2_
  11.5 2.4 %collective-permute-done.2.refs_3_ = bf16[16,1536]{1,0:T(8,128)(2,1)S(1)} collective-permute-done((bf16[16,1536]{1,0:T(8,128)(2,1)S(1)}, bf16[16,1536]{1,0:T(8,128)(2,1)S(1)}, u32[]{:S(2)}, u32[]{:S(2)}) %collective-permute-start.2) | collective-permute-done | bytes 49184 | tf_op jit(solution)/shard_map/ppermute | solution.py:116
  13.9 1.6 %collective-permute-start.4 = (bf16[32,1536]{1,0:T(8,128)(2,1)S(1)}, bf16[32,1536]{1,0:T(8,128)(2,1)S(1)}, u32[]{:S(2)}, u32[]{:S(2)}) collective-permute-start(bf16[32,1536]{1,0:T(8,128)(2,1)S(1)} %get-tuple-element.25.refs_0_), channel_id=1, source_target_pairs={{0,2},{1,3},{2,0},{3,1},{4,6},{5,7},{6,4},{7,5},{8,10},{9,11},{10,... | collective-permute-start | bytes 294920 | tf_op jit(solution)/shard_map/ppermute | solution.py:116
  15.4 0.0 collective-permute-start.3
  15.4 3.1 %collective-permute-done.4.refs_2_ = bf16[32,1536]{1,0:T(8,128)(2,1)S(1)} collective-permute-done((bf16[32,1536]{1,0:T(8,128)(2,1)S(1)}, bf16[32,1536]{1,0:T(8,128)(2,1)S(1)}, u32[]{:S(2)}, u32[]{:S(2)}) %collective-permute-start.4) | collective-permute-done | bytes 98336 | tf_op jit(solution)/shard_map/ppermute | solution.py:116
  18.5 0.0 collective-permute-start.5
  18.5 0.0 collective-permute-done.3.refs_1_
  18.5 5.0 %collective-permute-done.5.refs_3_ = bf16[32,1536]{1,0:T(8,128)(2,1)S(1)} collective-permute-done((bf16[32,1536]{1,0:T(8,128)(2,1)S(1)}, bf16[32,1536]{1,0:T(8,128)(2,1)S(1)}, u32[]{:S(2)}, u32[]{:S(2)}) %collective-permute-start.5) | collective-permute-done | bytes 98336 | tf_op jit(solution)/shard_map/ppermute | solution.py:116
  23.6 0.0 collective-permute-done.7.refs_8_
  23.6 0.0 collective-permute-done.6.refs_6_
  23.6 0.0 copy-start
  23.6 4.1 %shard_map.97.refs_4_ = bf16[128,1536]{1,0:T(8,128)(2,1)S(1)} custom-call(bf16[32,1536]{1,0:T(8,128)(2,1)S(1)} %get-tuple-element.25.refs_0_, bf16[32,1536]{1,0:T(8,128)(2,1)S(1)} %collective-permute-done.3.refs_1_, bf16[32,1536]{1,0:T(8,128)(2,1)S(1)} %collective-permute-done.4.refs_2_, bf16[32,1536]{1,0:T(8,128)(2,1)S(1)} %collective-permute-done.5.refs_3_, ...), custom_call_target="tpu_custom_call" | custom-call | tf_op jit(solution)/shard_map/pallas_call | solution.py:372
  27.7 0.7 %collective-permute-start.8 = (bf16[128,1536]{1,0:T(8,128)(2,1)S(1)}, bf16[128,1536]{1,0:T(8,128)(2,1)S(1)}, u32[]{:S(2)}, u32[]{:S(2)}) collective-permute-start(bf16[128,1536]{1,0:T(8,128)(2,1)S(1)} %shard_map.97.refs_4_), channel_id=1, source_target_pairs={{0,2},{2,0},{1,3},{3,1},{4,6},{6,4},{5,7},{7,5},{8,10},{10,8},{9,1... | collective-permute-start | bytes 1179656 | tf_op jit(solution)/shard_map/ppermute | solution.py:116
  28.4 0.0 collective-permute-start.10
  28.4 1.2 %collective-permute-done.10.refs_10_ = f32[7,256]{1,0:T(8,128)S(1)} collective-permute-done((f32[7,256]{1,0:T(8,128)S(1)}, f32[7,256]{1,0:T(8,128)S(1)}, u32[]{:S(2)}, u32[]{:S(2)}) %collective-permute-start.10) | collective-permute-done | bytes 7200 | tf_op jit(solution)/shard_map/ppermute | solution.py:116
  29.6 0.0 collective-permute-done.9.refs_8_
  29.6 9.3 %collective-permute-done.8.refs_5_ = bf16[128,1536]{1,0:T(8,128)(2,1)S(1)} collective-permute-done((bf16[128,1536]{1,0:T(8,128)(2,1)S(1)}, bf16[128,1536]{1,0:T(8,128)(2,1)S(1)}, u32[]{:S(2)}, u32[]{:S(2)}) %collective-permute-start.8) | collective-permute-done | bytes 393248 | tf_op jit(solution)/shard_map/ppermute | solution.py:116
  38.9 0.0 copy-done
  38.9 1.2 %shard_map.98 = (bf16[32,1536]{1,0:T(8,128)(2,1)S(1)}, bf16[32,1536]{1,0:T(8,128)(2,1)S(1)}, f32[16,128]{1,0:T(8,128)S(1)}) custom-call(bf16[32,1536]{1,0:T(8,128)(2,1)S(1)} %get-tuple-element.25.refs_0_, bf16[32,1536]{1,0:T(8,128)(2,1)S(1)} %collective-permute-done.3.refs_1_, bf16[32,1536]{1,0:T(8,128)(2,1)S(1)} %collective-permute-done.4.refs_2_, ...), custom_call_target="tpu_custom_call" | custom-call | tf_op jit(solution)/shard_map/pallas_call | solution.py:390
  40.2 0.0 collective-permute-start.11
  40.2 0.5 collective-permute-start.12
  40.7 0.3 collective-permute-start.13
  41.0 1.1 %collective-permute-start.14 = (f32[16,128]{1,0:T(8,128)S(1)}, f32[16,128]{1,0:T(8,128)S(1)}, u32[]{:S(2)}, u32[]{:S(2)}) collective-permute-start(f32[16,128]{1,0:T(8,128)S(1)} %get-tuple-element.33.refs_0_), channel_id=1, source_target_pairs={{0,3},{1,2},{2,1},{3,0},{4,7},{5,6},{6,5},{7,4},{8,11},{9,10},{10,... | collective-permute-start | bytes 24584 | tf_op jit(solution)/shard_map/ppermute | solution.py:116
  42.1 0.0 collective-permute-done.12.refs_1_
  42.1 2.3 %collective-permute-done.13.refs_2_ = f32[16,128]{1,0:T(8,128)S(1)} collective-permute-done((f32[16,128]{1,0:T(8,128)S(1)}, f32[16,128]{1,0:T(8,128)S(1)}, u32[]{:S(2)}, u32[]{:S(2)}) %collective-permute-start.13) | collective-permute-done | bytes 8224 | tf_op jit(solution)/shard_map/ppermute | solution.py:116
  44.4 0.0 collective-permute-done.14.refs_3_
  44.4 0.0 collective-permute-done.11.arrived_ref
  44.4 0.1 collective-permute-start.15
  44.5 4.1 %collective-permute-start.16 = (bf16[16,1792]{1,0:T(8,128)(2,1)S(1)}, bf16[16,1792]{1,0:T(8,128)(2,1)S(1)}, u32[]{:S(2)}, u32[]{:S(2)}) collective-permute-start(bf16[16,1792]{1,0:T(8,128)(2,1)S(1)} %get-tuple-element.36), channel_id=1, source_target_pairs={{0,8},{4,12},{8,0},{12,4},{1,9},{5,13},{9,1},{13,5},{2,10},{6,14},... | collective-permute-start | bytes 172040 | tf_op jit(solution)/shard_map/ppermute | solution.py:116
  48.5 0.3 collective-permute-start.17
  48.8 0.0 collective-permute-done.15.refs_1_
  48.9 3.2 %collective-permute-done.16.refs_2_ = bf16[16,1792]{1,0:T(8,128)(2,1)S(1)} collective-permute-done((bf16[16,1792]{1,0:T(8,128)(2,1)S(1)}, bf16[16,1792]{1,0:T(8,128)(2,1)S(1)}, u32[]{:S(2)}, u32[]{:S(2)}) %collective-permute-start.16) | collective-permute-done | bytes 57376 | tf_op jit(solution)/shard_map/ppermute | solution.py:116
  52.1 2.4 %collective-permute-done.17.refs_3_ = bf16[16,1792]{1,0:T(8,128)(2,1)S(1)} collective-permute-done((bf16[16,1792]{1,0:T(8,128)(2,1)S(1)}, bf16[16,1792]{1,0:T(8,128)(2,1)S(1)}, u32[]{:S(2)}, u32[]{:S(2)}) %collective-permute-start.17) | collective-permute-done | bytes 57376 | tf_op jit(solution)/shard_map/ppermute | solution.py:116
  54.5 0.7 %shard_map.100 = (bf16[64,1536]{1,0:T(8,128)(2,1)}, f32[7,2,15]{2,1,0:T(2,128)}) custom-call(bf16[16,1792]{1,0:T(8,128)(2,1)S(1)} %get-tuple-element.34.refs_0_, bf16[16,1792]{1,0:T(8,128)(2,1)S(1)} %collective-permute-done.15.refs_1_, bf16[16,1792]{1,0:T(8,128)(2,1)S(1)} %collective-permute-done.16.refs_2_, bf16[16,1792]{1,0:T(8,128)(2,1)S(1)} %collective-permute-done.17.refs_3_), custom_call_target="tpu_custom_call" | custom-call | tf_op jit(solution)/shard_map/pallas_call | solution.py:417
  (2 shorter events, 0.0 us)
Async XLA Ops:
  0.6 23.0 %collective-permute-start.6 = (bf16[1152,1536]{1,0:T(8,128)(2,1)}, bf16[1152,1536]{1,0:T(8,128)(2,1)S(1)}, u32[]{:S(2)}, u32[]{:S(2)}) collective-permute-start(bf16[1152,1536]{1,0:T(8,128)(2,1)} %bitcast.7), channel_id=1, source_target_pairs={{0,1},{1,0},{2,3},{3,2},{4,5},{5,4},{6,7},{7,6},{8,9},{9,8},{10,11... | collective-permute-start | bytes 10616840 | tf_op jit(solution)/shard_map/ppermute | solution.py:116
  1.2 22.4 %collective-permute-start.7 = (bf16[384,1536]{1,0:T(8,128)(2,1)}, bf16[384,1536]{1,0:T(8,128)(2,1)S(1)}, u32[]{:S(2)}, u32[]{:S(2)}) collective-permute-start(bf16[384,1536]{1,0:T(8,128)(2,1)} %refs_7_.2), channel_id=1, source_target_pairs={{0,1},{1,0},{2,3},{3,2},{4,5},{5,4},{6,7},{7,6},{8,9},{9,8},{10,11... | collective-permute-start | bytes 3538952 | tf_op jit(solution)/shard_map/ppermute | solution.py:116
  1.3 28.3 %collective-permute-start.9 = (bf16[2,1536,256]{2,1,0:T(8,128)(2,1)}, bf16[2,1536,256]{2,1,0:T(8,128)(2,1)S(1)}, u32[]{:S(2)}, u32[]{:S(2)}) collective-permute-start(bf16[2,1536,256]{2,1,0:T(8,128)(2,1)} %refs_7_.3), channel_id=1, source_target_pairs={{0,1},{1,0},{2,3},{3,2},{4,5},{5,4},{6,7},{7,6},{8,9},{9,8},{10,11... | collective-permute-start | bytes 4718600 | tf_op jit(solution)/shard_map/ppermute | solution.py:116
  2.7 5.3 %collective-permute-start = (bf16[16,1536]{1,0:T(8,128)(2,1)S(1)}, bf16[16,1536]{1,0:T(8,128)(2,1)S(1)}, u32[]{:S(2)}, u32[]{:S(2)}) collective-permute-start(bf16[16,1536]{1,0:T(8,128)(2,1)S(1)} %get-tuple-element.22), channel_id=1, source_target_pairs={{0,4},{4,0},{8,12},{12,8},{1,5},{5,1},{9,13},{13,9},{2,6},{6,2},{1... | collective-permute-start | bytes 147464 | tf_op jit(solution)/shard_map/ppermute | solution.py:116
  5.4 6.1 %collective-permute-start.1 = (bf16[16,1536]{1,0:T(8,128)(2,1)S(1)}, bf16[16,1536]{1,0:T(8,128)(2,1)S(1)}, u32[]{:S(2)}, u32[]{:S(2)}) collective-permute-start(bf16[16,1536]{1,0:T(8,128)(2,1)S(1)} %get-tuple-element.23), channel_id=1, source_target_pairs={{0,8},{4,12},{8,0},{12,4},{1,9},{5,13},{9,1},{13,5},{2,10},{6,14},... | collective-permute-start | bytes 147464 | tf_op jit(solution)/shard_map/ppermute | solution.py:116
  8.0 5.9 %collective-permute-start.2 = (bf16[16,1536]{1,0:T(8,128)(2,1)S(1)}, bf16[16,1536]{1,0:T(8,128)(2,1)S(1)}, u32[]{:S(2)}, u32[]{:S(2)}) collective-permute-start(bf16[16,1536]{1,0:T(8,128)(2,1)S(1)} %get-tuple-element.24), channel_id=1, source_target_pairs={{0,12},{4,8},{8,4},{12,0},{1,13},{5,9},{9,5},{13,1},{2,14},{6,10},... | collective-permute-start | bytes 147464 | tf_op jit(solution)/shard_map/ppermute | solution.py:116
  13.9 4.7 %collective-permute-start.4 = (bf16[32,1536]{1,0:T(8,128)(2,1)S(1)}, bf16[32,1536]{1,0:T(8,128)(2,1)S(1)}, u32[]{:S(2)}, u32[]{:S(2)}) collective-permute-start(bf16[32,1536]{1,0:T(8,128)(2,1)S(1)} %get-tuple-element.25.refs_0_), channel_id=1, source_target_pairs={{0,2},{1,3},{2,0},{3,1},{4,6},{5,7},{6,4},{7,5},{8,10},{9,11},{10,... | collective-permute-start | bytes 294920 | tf_op jit(solution)/shard_map/ppermute | solution.py:116
  15.4 3.1 %collective-permute-start.3 = (bf16[32,1536]{1,0:T(8,128)(2,1)S(1)}, bf16[32,1536]{1,0:T(8,128)(2,1)S(1)}, u32[]{:S(2)}, u32[]{:S(2)}) collective-permute-start(bf16[32,1536]{1,0:T(8,128)(2,1)S(1)} %get-tuple-element.26), channel_id=1, source_target_pairs={{0,1},{1,0},{2,3},{3,2},{4,5},{5,4},{6,7},{7,6},{8,9},{9,8},{10,11... | collective-permute-start | bytes 294920 | tf_op jit(solution)/shard_map/ppermute | solution.py:116
  18.5 5.1 %collective-permute-start.5 = (bf16[32,1536]{1,0:T(8,128)(2,1)S(1)}, bf16[32,1536]{1,0:T(8,128)(2,1)S(1)}, u32[]{:S(2)}, u32[]{:S(2)}) collective-permute-start(bf16[32,1536]{1,0:T(8,128)(2,1)S(1)} %get-tuple-element.26), channel_id=1, source_target_pairs={{0,3},{1,2},{2,1},{3,0},{4,7},{5,6},{6,5},{7,4},{8,11},{9,10},{10,... | collective-permute-start | bytes 294920 | tf_op jit(solution)/shard_map/ppermute | solution.py:116
  23.6 15.3 %copy-start = (bf16[2,1536,256]{2,1,0:T(8,128)(2,1)S(1)}, bf16[2,1536,256]{2,1,0:T(8,128)(2,1)}, u32[]{:S(2)}) copy-start(bf16[2,1536,256]{2,1,0:T(8,128)(2,1)} %refs_7_.3) | copy-start | bytes 4718596
  27.7 11.2 %collective-permute-start.8 = (bf16[128,1536]{1,0:T(8,128)(2,1)S(1)}, bf16[128,1536]{1,0:T(8,128)(2,1)S(1)}, u32[]{:S(2)}, u32[]{:S(2)}) collective-permute-start(bf16[128,1536]{1,0:T(8,128)(2,1)S(1)} %shard_map.97.refs_4_), channel_id=1, source_target_pairs={{0,2},{2,0},{1,3},{3,1},{4,6},{6,4},{5,7},{7,5},{8,10},{10,8},{9,1... | collective-permute-start | bytes 1179656 | tf_op jit(solution)/shard_map/ppermute | solution.py:116
  28.4 1.2 %collective-permute-start.10 = (f32[7,256]{1,0:T(8,128)S(1)}, f32[7,256]{1,0:T(8,128)S(1)}, u32[]{:S(2)}, u32[]{:S(2)}) collective-permute-start(f32[7,256]{1,0:T(8,128)S(1)} %get-tuple-element.29.refs_9_), channel_id=1, source_target_pairs={{0,1},{1,0},{2,3},{3,2},{4,5},{5,4},{6,7},{7,6},{8,9},{9,8},{10,11... | collective-permute-start | bytes 21512 | tf_op jit(solution)/shard_map/ppermute | solution.py:116
  40.2 4.2 %collective-permute-start.11 = (bf16[32,1536]{1,0:T(8,128)(2,1)S(1)}, bf16[32,1536]{1,0:T(8,128)(2,1)S(1)}, u32[]{:S(2)}, u32[]{:S(2)}) collective-permute-start(bf16[32,1536]{1,0:T(8,128)(2,1)S(1)} %get-tuple-element.32), channel_id=1, source_target_pairs={{0,1},{1,0},{2,3},{3,2},{4,5},{5,4},{6,7},{7,6},{8,9},{9,8},{10,11... | collective-permute-start | bytes 294920 | tf_op jit(solution)/shard_map/ppermute | solution.py:116
  40.2 1.9 %collective-permute-start.12 = (f32[16,128]{1,0:T(8,128)S(1)}, f32[16,128]{1,0:T(8,128)S(1)}, u32[]{:S(2)}, u32[]{:S(2)}) collective-permute-start(f32[16,128]{1,0:T(8,128)S(1)} %get-tuple-element.33.refs_0_), channel_id=1, source_target_pairs={{0,1},{1,0},{2,3},{3,2},{4,5},{5,4},{6,7},{7,6},{8,9},{9,8},{10,11... | collective-permute-start | bytes 24584 | tf_op jit(solution)/shard_map/ppermute | solution.py:116
  40.7 3.7 %collective-permute-start.13 = (f32[16,128]{1,0:T(8,128)S(1)}, f32[16,128]{1,0:T(8,128)S(1)}, u32[]{:S(2)}, u32[]{:S(2)}) collective-permute-start(f32[16,128]{1,0:T(8,128)S(1)} %get-tuple-element.33.refs_0_), channel_id=1, source_target_pairs={{0,2},{1,3},{2,0},{3,1},{4,6},{5,7},{6,4},{7,5},{8,10},{9,11},{10,... | collective-permute-start | bytes 24584 | tf_op jit(solution)/shard_map/ppermute | solution.py:116
  41.0 3.4 %collective-permute-start.14 = (f32[16,128]{1,0:T(8,128)S(1)}, f32[16,128]{1,0:T(8,128)S(1)}, u32[]{:S(2)}, u32[]{:S(2)}) collective-permute-start(f32[16,128]{1,0:T(8,128)S(1)} %get-tuple-element.33.refs_0_), channel_id=1, source_target_pairs={{0,3},{1,2},{2,1},{3,0},{4,7},{5,6},{6,5},{7,4},{8,11},{9,10},{10,... | collective-permute-start | bytes 24584 | tf_op jit(solution)/shard_map/ppermute | solution.py:116
  44.4 4.5 %collective-permute-start.15 = (bf16[16,1792]{1,0:T(8,128)(2,1)S(1)}, bf16[16,1792]{1,0:T(8,128)(2,1)S(1)}, u32[]{:S(2)}, u32[]{:S(2)}) collective-permute-start(bf16[16,1792]{1,0:T(8,128)(2,1)S(1)} %get-tuple-element.35), channel_id=1, source_target_pairs={{0,4},{4,0},{8,12},{12,8},{1,5},{5,1},{9,13},{13,9},{2,6},{6,2},{1... | collective-permute-start | bytes 172040 | tf_op jit(solution)/shard_map/ppermute | solution.py:116
  44.5 7.6 %collective-permute-start.16 = (bf16[16,1792]{1,0:T(8,128)(2,1)S(1)}, bf16[16,1792]{1,0:T(8,128)(2,1)S(1)}, u32[]{:S(2)}, u32[]{:S(2)}) collective-permute-start(bf16[16,1792]{1,0:T(8,128)(2,1)S(1)} %get-tuple-element.36), channel_id=1, source_target_pairs={{0,8},{4,12},{8,0},{12,4},{1,9},{5,13},{9,1},{13,5},{2,10},{6,14},... | collective-permute-start | bytes 172040 | tf_op jit(solution)/shard_map/ppermute | solution.py:116
  48.5 6.0 %collective-permute-start.17 = (bf16[16,1792]{1,0:T(8,128)(2,1)S(1)}, bf16[16,1792]{1,0:T(8,128)(2,1)S(1)}, u32[]{:S(2)}, u32[]{:S(2)}) collective-permute-start(bf16[16,1792]{1,0:T(8,128)(2,1)S(1)} %get-tuple-element.37), channel_id=1, source_target_pairs={{0,12},{4,8},{8,4},{12,0},{1,13},{5,9},{9,5},{13,1},{2,14},{6,10},... | collective-permute-start | bytes 172040 | tf_op jit(solution)/shard_map/ppermute | solution.py:116

commit v2 on v1

--- a/solution.py
+++ b/solution.py
@@ -178,12 +178,13 @@
         fetch(index).start()
     fetch_out = pltpu.make_async_copy(wo_far, wo_own, sems.at[heads // group])
     fetch_out.start()
-    step = token_refs[0].shape[0]
     gain_row = lined(gain_ref)
-    for place, ref in enumerate(token_refs):
-        normed_ref[place * step : (place + 1) * step, :] = scaled(
+    first = 0
+    for ref in token_refs:
+        normed_ref[first : first + ref.shape[0], :] = scaled(
             ref[...].astype(jnp.float32), gain_row
         )
+        first += ref.shape[0]
     rows = normed_ref.shape[0]
 
     def project(wq_ref, source, size, target):
@@ -231,23 +232,29 @@
     out_ref[...] = total.astype(jnp.bfloat16)
 
 
-def pair_kernel(cols, frames, seq_count, split_count, patches, others, *refs):
-    token_refs, refs = refs[:split_count], refs[split_count:]
+def pair_kernel(cols, frames, order, split_count, patches, others, *refs):
+    batches = 2 * split_count
+    token_refs, refs = refs[:batches], refs[batches:]
     own_ref, refs = refs[0], refs[1:]
     other_refs, refs = refs[:others], refs[others:]
     gain_ref, wp_a, wp_b, wa_a, wa_b, pairs_ref, keep_ref, pass_ref, part_ref, *refs = refs
     hidden_ref, cur_ref, fol_ref = refs
-    step = token_refs[0].shape[0]
+    seq_count = len(order)
+    step = seq_count * cols
     seq_place = lax.axis_index("seq")
     split_place = lax.axis_index(("head", "sub"))
     roll = (seq_place * 2 + lax.axis_index("sub")) * cols // patches
-    for place, ref in enumerate(token_refs):
-        rows = slice(place * step, (place + 1) * step)
-        branch = own_ref[rows, :].astype(jnp.float32)
-        for index, other in enumerate(other_refs):
-            there = place ^ (2 * (index + 1))
-            branch = branch + other[there * step : (there + 1) * step, :].astype(jnp.float32)
-        hidden_ref[rows, :] = (ref[...].astype(jnp.float32) + branch).astype(jnp.bfloat16)
+    for place in range(split_count):
+        first = place * step
+        for ref in token_refs[2 * place : 2 * place + 2]:
+            height = ref.shape[0]
+            rows = slice(first, first + height)
+            branch = own_ref[rows, :].astype(jnp.float32)
+            for index, other in enumerate(other_refs):
+                there = first + ((place ^ (2 * (index + 1))) - place) * step
+                branch = branch + other[there : there + height, :].astype(jnp.float32)
+            hidden_ref[rows, :] = (ref[...].astype(jnp.float32) + branch).astype(jnp.bfloat16)
+            first += height
     keep_ref[...] = hidden_ref[:step, :]
     pass_ref[...] = hidden_ref[step : 2 * step, :]
     vit = scaled(hidden_ref[...].astype(jnp.float32), lined(gain_ref))
@@ -256,9 +263,10 @@
         current = jnp.dot(vit, wp_ref[0], preferred_element_type=jnp.float32)
         ahead = jnp.dot(vit, wp_ref[1], preferred_element_type=jnp.float32)
         for split in range(split_count):
-            for seq in range(seq_count):
+            for index, seq in enumerate(order):
                 frame = (seq_place ^ seq) * split_count + (split_place ^ split)
-                piece = slice((split * seq_count + seq) * cols, (split * seq_count + seq + 1) * cols)
+                first = (split * seq_count + index) * cols
+                piece = slice(first, first + cols)
                 place = pl.ds(pl.multiple_of(frame * cols, cols), cols)
                 cur_ref[place, :] = current[piece, :]
                 fol_ref[place, :] = ahead[piece, :]
@@ -283,7 +291,7 @@
         )
 
 
-def pack_kernel(cols, parts, kept_ref, arrived_ref, *refs):
+def pack_kernel(cols, order, parts, kept_ref, arrived_ref, *refs):
     part_refs, block_refs = refs[:parts], refs[parts:]
     width = kept_ref.shape[1]
     total = part_refs[0][...]
@@ -301,8 +309,9 @@
 
         @pl.when(lax.axis_index("sub") == 1 - lower)
         def _():
-            for step, block_ref in enumerate(block_refs):
-                rows = slice(step * cols, (step + 1) * cols)
+            for index, step in enumerate(order):
+                block_ref = block_refs[step]
+                rows = slice(index * cols, (index + 1) * cols)
                 block_ref[:cols, :width] = first_ref[rows, :]
                 block_ref[cols:, :width] = second_ref[rows, :]
 
@@ -350,29 +359,39 @@
     )(off_chip(frames_in), *[off_chip(value) for value in small])
     pieces = cut[:seq_count]
     attn_gain, vit_gain, wa_own, pair_frames = cut[seq_count:]
-    pieces = [pieces[0]] + [swap(pieces[step], "seq", step) for step in range(1, seq_count)]
+    cut_pieces = pieces
+    pieces = [cut_pieces[0]]
+    for step in range(1, seq_count):
+        pieces.append(swap(cut_pieces[step], "seq", step))
     wq_pal = swap(wq_own, "sub", 1)
     wo_pal = swap(w_out, "sub", 1)
     wp_pal = swap(w_pair, "sub", 1)
     wa_pal = swap(wa_own, "sub", 1)
     half = pltpu.VMEM((seq_count * cols, width), jnp.bfloat16)
-    mine, pals = pl.pallas_call(
-        functools.partial(halve_kernel, cols),
-        compiler_params=GRANT,
-        in_specs=[vmem] * seq_count,
-        out_specs=[vmem] * 2,
-        out_shape=[half] * 2,
-    )(*pieces)
-    tokens = [mine] + [
-        swap(pals if step & 1 else mine, ("head", "sub"), step)
-        for step in range(1, split_count)
-    ]
+    middle = seq_count // 2
+    early = (0, middle) if seq_count > 2 else (0,)
+    late = tuple(step for step in range(1, seq_count) if step not in early)
+    order = early + late
+    batches = []
+    for steps in (early, late):
+        mine, pals = pl.pallas_call(
+            functools.partial(halve_kernel, cols),
+            compiler_params=GRANT,
+            in_specs=[vmem] * len(steps),
+            out_specs=[vmem] * 2,
+            out_shape=[pltpu.VMEM((len(steps) * cols, width), jnp.bfloat16)] * 2,
+        )(*[pieces[step] for step in steps])
+        batch = [mine]
+        for step in range(1, split_count):
+            batch.append(swap(pals if step & 1 else mine, ("head", "sub"), step))
+        batches.append(batch)
+    tokens = [batch[step] for step in range(split_count) for batch in batches]
     rows = split_count * seq_count * cols
     inner = heads * head_dim
     branch = pl.pallas_call(
         functools.partial(attend_kernel, cols, heads, head_dim),
         compiler_params=GRANT,
-        in_specs=[vmem] * (split_count + 1) + [hbm, vmem, hbm, vmem],
+        in_specs=[vmem] * (2 * split_count + 1) + [hbm, vmem, hbm, vmem],
         out_specs=vmem,
         out_shape=pltpu.VMEM((rows, width), jnp.bfloat16),
         scratch_shapes=[
@@ -389,10 +408,10 @@
     wanted = pair_frames.shape[1]
     kept, passed, part = pl.pallas_call(
         functools.partial(
-            pair_kernel, cols, F, seq_count, split_count, patches, head_count - 1
+            pair_kernel, cols, F, order, split_count, patches, head_count - 1
         ),
         compiler_params=GRANT,
-        in_specs=[vmem] * (split_count + head_count + 6),
+        in_specs=[vmem] * (2 * split_count + head_count + 6),
         out_specs=[vmem] * 3,
         out_shape=(half, half, pltpu.VMEM((ROLLS * LINES, 128), jnp.float32)),
         scratch_shapes=[
@@ -405,15 +424,20 @@
         wa_own, wa_pal, pair_frames,
     )
     arrived = swap(passed, "sub", 1)
-    parts = [part] + [swap(part, ("head", "sub"), step) for step in range(1, split_count)]
+    parts = [part]
+    for step in range(1, split_count):
+        parts.append(swap(part, ("head", "sub"), step))
     blocks = pl.pallas_call(
-        functools.partial(pack_kernel, cols, split_count),
+        functools.partial(pack_kernel, cols, order, split_count),
         compiler_params=GRANT,
         in_specs=[vmem] * (2 + split_count),
         out_specs=[vmem] * seq_count,
         out_shape=[pltpu.VMEM((wide, width + 256), jnp.bfloat16)] * seq_count,
     )(kept, arrived, *parts)
-    blocks = [blocks[0]] + [swap(blocks[step], "seq", step) for step in range(1, seq_count)]
+    cut_blocks = blocks
+    blocks = [cut_blocks[0]]
+    for step in range(1, seq_count):
+        blocks.append(swap(cut_blocks[step], "seq", step))
     hidden, actions = pl.pallas_call(
         functools.partial(place_kernel, seq_count, wide),
         compiler_params=GRANT,

time: 55.4 us -> 57.1 us (1.031)
  starting transfers between devices: 18.5 us -> 21.7 us
  waiting for transfers between devices: 29 us -> 27.5 us
    ppermute x18 -> x21, starting transfers between devices: 18.5 us -> 21.7 us  [swap(): return on_chip(lax.ppermute(value, axis, pairs))]
    ppermute x18 -> x21, waiting for transfers between devices: 29 us -> 27.5 us  [swap(): return on_chip(lax.ppermute(value, axis, pairs))]
  transfers between devices with their start and end apart: 18 -> 21, of which waited for: 8 -> 11; matrix products, arithmetic and copies ran while one was open for 0% -> 0% of each run, Pallas kernels for 9% -> 9%
where the time goes in v2:
time: 57.1 us; the launch traced here: 56.9 us
  waiting for transfers between devices  27.5 us (48%)
  starting transfers between devices  21.7 us (38%)
  Pallas kernels  7.03 us (12%)
  between operations  0.68 us (1%)
    ppermute x21, waiting for transfers between devices, swap(): return on_chip(lax.ppermute(value, axis, pairs))  27.5 us
    ppermute x21, starting transfers between devices, swap(): return on_chip(lax.ppermute(value, axis, pairs))  21.7 us
    pallas_call x1, Pallas kernels, fast_shards(): pl.pallas_call(functools.partial(attend_kernel, cols, heads, head_dim), c...  4.11 us
    pallas_call x1, Pallas kernels, fast_shards(): pl.pallas_call(functools.partial(pair_kernel, cols, F, order, split_count...  1.23 us
  transfers between devices with their start and end apart: 21, of which 11 were waited for; matrix products, arithmetic and copies ran while one was open for 0% of the time, Pallas kernels for 9%

profile of v2, /device:TPU:0, one launch (start us, length us, event | category | flops | bytes accessed | tf_op | source)
XLA Modules:
  0.0 56.9 jit_solution(12706342297578026775)
XLA Ops:
  0.6 0.6 collective-permute-start.9
  1.2 0.1 collective-permute-start.10
  1.3 0.4 collective-permute-start.12
  1.7 0.9 %shard_map.95 = (bf16[16,1536]{1,0:T(8,128)(2,1)S(1)}, bf16[16,1536]{1,0:T(8,128)(2,1)S(1)}, bf16[16,1536]{1,0:T(8,128)(2,1)S(1)}, bf16[16,1536]{1,0:T(8,128)(2,...) custom-call(bf16[64,1536]{1,0:T(8,128)(2,1)} %tokens_ref.1, ...), custom_call_target="tpu_custom_call" | custom-call | tf_op jit(solution)/shard_map/pallas_call | solution.py:351
  2.7 2.7 %collective-permute-start.1 = (bf16[16,1536]{1,0:T(8,128)(2,1)S(1)}, bf16[16,1536]{1,0:T(8,128)(2,1)S(1)}, u32[]{:S(2)}, u32[]{:S(2)}) collective-permute-start(bf16[16,1536]{1,0:T(8,128)(2,1)S(1)} %get-tuple-element.26), channel_id=1, source_target_pairs={{0,4},{4,0},{8,12},{12,8},{1,5},{5,1},{9,13},{13,9},{2,6},{6,2},{1... | collective-permute-start | bytes 147464 | tf_op jit(solution)/shard_map/ppermute | solution.py:116
  5.4 2.5 %collective-permute-start.2 = (bf16[16,1536]{1,0:T(8,128)(2,1)S(1)}, bf16[16,1536]{1,0:T(8,128)(2,1)S(1)}, u32[]{:S(2)}, u32[]{:S(2)}) collective-permute-start(bf16[16,1536]{1,0:T(8,128)(2,1)S(1)} %get-tuple-element.27), channel_id=1, source_target_pairs={{0,12},{4,8},{8,4},{12,0},{1,13},{5,9},{9,5},{13,1},{2,14},{6,10},... | collective-permute-start | bytes 147464 | tf_op jit(solution)/shard_map/ppermute | solution.py:116
  7.8 0.0 collective-permute-done.1.refs_0_
  7.8 2.6 %collective-permute-start = (bf16[16,1536]{1,0:T(8,128)(2,1)S(1)}, bf16[16,1536]{1,0:T(8,128)(2,1)S(1)}, u32[]{:S(2)}, u32[]{:S(2)}) collective-permute-start(bf16[16,1536]{1,0:T(8,128)(2,1)S(1)} %get-tuple-element.24), channel_id=1, source_target_pairs={{0,8},{4,12},{8,0},{12,4},{1,9},{5,13},{9,1},{13,5},{2,10},{6,14},... | collective-permute-start | bytes 147464 | tf_op jit(solution)/shard_map/ppermute | solution.py:116
  10.5 0.8 %collective-permute-done.2.refs_1_ = bf16[16,1536]{1,0:T(8,128)(2,1)S(1)} collective-permute-done((bf16[16,1536]{1,0:T(8,128)(2,1)S(1)}, bf16[16,1536]{1,0:T(8,128)(2,1)S(1)}, u32[]{:S(2)}, u32[]{:S(2)}) %collective-permute-start.2) | collective-permute-done | bytes 49184 | tf_op jit(solution)/shard_map/ppermute | solution.py:116
  11.3 1.6 %collective-permute-start.6 = (bf16[16,1536]{1,0:T(8,128)(2,1)S(1)}, bf16[16,1536]{1,0:T(8,128)(2,1)S(1)}, u32[]{:S(2)}, u32[]{:S(2)}) collective-permute-start(bf16[16,1536]{1,0:T(8,128)(2,1)S(1)} %get-tuple-element.28.refs_1_), channel_id=1, source_target_pairs={{0,2},{1,3},{2,0},{3,1},{4,6},{5,7},{6,4},{7,5},{8,10},{9,11},{10,... | collective-permute-start | bytes 147464 | tf_op jit(solution)/shard_map/ppermute | solution.py:116
  12.8 0.0 collective-permute-done.refs_1_
  12.8 1.6 %collective-permute-start.5 = (bf16[16,1536]{1,0:T(8,128)(2,1)S(1)}, bf16[16,1536]{1,0:T(8,128)(2,1)S(1)}, u32[]{:S(2)}, u32[]{:S(2)}) collective-permute-start(bf16[16,1536]{1,0:T(8,128)(2,1)S(1)} %get-tuple-element.25.refs_0_), channel_id=1, source_target_pairs={{0,2},{1,3},{2,0},{3,1},{4,6},{5,7},{6,4},{7,5},{8,10},{9,11},{10,... | collective-permute-start | bytes 147464 | tf_op jit(solution)/shard_map/ppermute | solution.py:116
  14.4 1.4 %collective-permute-done.6.refs_5_ = bf16[16,1536]{1,0:T(8,128)(2,1)S(1)} collective-permute-done((bf16[16,1536]{1,0:T(8,128)(2,1)S(1)}, bf16[16,1536]{1,0:T(8,128)(2,1)S(1)}, u32[]{:S(2)}, u32[]{:S(2)}) %collective-permute-start.6) | collective-permute-done | bytes 49184 | tf_op jit(solution)/shard_map/ppermute | solution.py:116
  15.8 0.0 collective-permute-start.4
  15.8 1.1 %collective-permute-done.5.refs_4_ = bf16[16,1536]{1,0:T(8,128)(2,1)S(1)} collective-permute-done((bf16[16,1536]{1,0:T(8,128)(2,1)S(1)}, bf16[16,1536]{1,0:T(8,128)(2,1)S(1)}, u32[]{:S(2)}, u32[]{:S(2)}) %collective-permute-start.5) | collective-permute-done | bytes 49184 | tf_op jit(solution)/shard_map/ppermute | solution.py:116
  17.0 0.5 collective-permute-start.8
  17.5 0.0 collective-permute-done.4.refs_3_
  17.5 1.2 %collective-permute-start.3 = (bf16[16,1536]{1,0:T(8,128)(2,1)S(1)}, bf16[16,1536]{1,0:T(8,128)(2,1)S(1)}, u32[]{:S(2)}, u32[]{:S(2)}) collective-permute-start(bf16[16,1536]{1,0:T(8,128)(2,1)S(1)} %get-tuple-element.29), channel_id=1, source_target_pairs={{0,1},{1,0},{2,3},{3,2},{4,5},{5,4},{6,7},{7,6},{8,9},{9,8},{10,11... | collective-permute-start | bytes 147464 | tf_op jit(solution)/shard_map/ppermute | solution.py:116
  18.6 2.3 %collective-permute-done.8.refs_7_ = bf16[16,1536]{1,0:T(8,128)(2,1)S(1)} collective-permute-done((bf16[16,1536]{1,0:T(8,128)(2,1)S(1)}, bf16[16,1536]{1,0:T(8,128)(2,1)S(1)}, u32[]{:S(2)}, u32[]{:S(2)}) %collective-permute-start.8) | collective-permute-done | bytes 49184 | tf_op jit(solution)/shard_map/ppermute | solution.py:116
  21.0 0.3 collective-permute-start.7
  21.3 0.0 collective-permute-done.3.refs_2_
  21.3 3.4 %collective-permute-done.7.refs_6_ = bf16[16,1536]{1,0:T(8,128)(2,1)S(1)} collective-permute-done((bf16[16,1536]{1,0:T(8,128)(2,1)S(1)}, bf16[16,1536]{1,0:T(8,128)(2,1)S(1)}, u32[]{:S(2)}, u32[]{:S(2)}) %collective-permute-start.7) | collective-permute-done | bytes 49184 | tf_op jit(solution)/shard_map/ppermute | solution.py:116
  24.7 0.0 collective-permute-done.10.refs_12_
  24.7 0.0 collective-permute-done.9.refs_10_
  24.7 0.0 copy-start
  24.7 4.1 %shard_map.98.refs_8_ = bf16[128,1536]{1,0:T(8,128)(2,1)S(1)} custom-call(bf16[16,1536]{1,0:T(8,128)(2,1)S(1)} %get-tuple-element.25.refs_0_, bf16[16,1536]{1,0:T(8,128)(2,1)S(1)} %get-tuple-element.28.refs_1_, bf16[16,1536]{1,0:T(8,128)(2,1)S(1)} %collective-permute-done.3.refs_2_, bf16[16,1536]{1,0:T(8,128)(2,1)S(1)} %collective-permute-done.4.refs_3_, ...), custom_call_target="tpu_custom_call" | custom-call | tf_op jit(solution)/shard_map/pallas_call | solution.py:391
  28.8 1.3 %collective-permute-start.11 = (bf16[128,1536]{1,0:T(8,128)(2,1)S(1)}, bf16[128,1536]{1,0:T(8,128)(2,1)S(1)}, u32[]{:S(2)}, u32[]{:S(2)}) collective-permute-start(bf16[128,1536]{1,0:T(8,128)(2,1)S(1)} %shard_map.98.refs_8_), channel_id=1, source_target_pairs={{0,2},{2,0},{1,3},{3,1},{4,6},{6,4},{5,7},{7,5},{8,10},{10,8},{9,1... | collective-permute-start | bytes 1179656 | tf_op jit(solution)/shard_map/ppermute | solution.py:116
  30.1 0.0 collective-permute-start.13
  30.1 1.2 %collective-permute-done.13.refs_14_ = f32[7,256]{1,0:T(8,128)S(1)} collective-permute-done((f32[7,256]{1,0:T(8,128)S(1)}, f32[7,256]{1,0:T(8,128)S(1)}, u32[]{:S(2)}, u32[]{:S(2)}) %collective-permute-start.13) | collective-permute-done | bytes 7200 | tf_op jit(solution)/shard_map/ppermute | solution.py:116
  31.3 0.0 collective-permute-done.12.refs_12_
  31.3 8.7 %collective-permute-done.11.refs_9_ = bf16[128,1536]{1,0:T(8,128)(2,1)S(1)} collective-permute-done((bf16[128,1536]{1,0:T(8,128)(2,1)S(1)}, bf16[128,1536]{1,0:T(8,128)(2,1)S(1)}, u32[]{:S(2)}, u32[]{:S(2)}) %collective-permute-start.11) | collective-permute-done | bytes 393248 | tf_op jit(solution)/shard_map/ppermute | solution.py:116
  40.1 0.0 copy-done
  40.1 1.2 %shard_map.99 = (bf16[32,1536]{1,0:T(8,128)(2,1)S(1)}, bf16[32,1536]{1,0:T(8,128)(2,1)S(1)}, f32[16,128]{1,0:T(8,128)S(1)}) custom-call(bf16[16,1536]{1,0:T(8,128)(2,1)S(1)} %get-tuple-element.25.refs_0_, bf16[16,1536]{1,0:T(8,128)(2,1)S(1)} %get-tuple-element.28.refs_1_, bf16[16,1536]{1,0:T(8,128)(2,1)S(1)} %collective-permute-done.3.refs_2_, ...), custom_call_target="tpu_custom_call" | custom-call | tf_op jit(solution)/shard_map/pallas_call | solution.py:409
  41.3 0.0 collective-permute-start.14
  41.3 0.5 collective-permute-start.15
  41.8 1.0 %collective-permute-start.16 = (f32[16,128]{1,0:T(8,128)S(1)}, f32[16,128]{1,0:T(8,128)S(1)}, u32[]{:S(2)}, u32[]{:S(2)}) collective-permute-start(f32[16,128]{1,0:T(8,128)S(1)} %get-tuple-element.37.refs_0_), channel_id=1, source_target_pairs={{0,2},{1,3},{2,0},{3,1},{4,6},{5,7},{6,4},{7,5},{8,10},{9,11},{10,... | collective-permute-start | bytes 24584 | tf_op jit(solution)/shard_map/ppermute | solution.py:116
  42.8 0.4 collective-permute-start.17
  43.2 0.0 collective-permute-done.15.refs_1_
  43.2 2.3 %collective-permute-done.16.refs_2_ = f32[16,128]{1,0:T(8,128)S(1)} collective-permute-done((f32[16,128]{1,0:T(8,128)S(1)}, f32[16,128]{1,0:T(8,128)S(1)}, u32[]{:S(2)}, u32[]{:S(2)}) %collective-permute-start.16) | collective-permute-done | bytes 8224 | tf_op jit(solution)/shard_map/ppermute | solution.py:116
  45.5 0.5 collective-permute-done.17.refs_3_
  45.9 0.0 collective-permute-done.14.arrived_ref
  46.0 1.3 %collective-permute-start.18 = (bf16[16,1792]{1,0:T(8,128)(2,1)S(1)}, bf16[16,1792]{1,0:T(8,128)(2,1)S(1)}, u32[]{:S(2)}, u32[]{:S(2)}) collective-permute-start(bf16[16,1792]{1,0:T(8,128)(2,1)S(1)} %get-tuple-element.39), channel_id=1, source_target_pairs={{0,4},{4,0},{8,12},{12,8},{1,5},{5,1},{9,13},{13,9},{2,6},{6,2},{1... | collective-permute-start | bytes 172040 | tf_op jit(solution)/shard_map/ppermute | solution.py:116
  47.2 3.0 %collective-permute-start.19 = (bf16[16,1792]{1,0:T(8,128)(2,1)S(1)}, bf16[16,1792]{1,0:T(8,128)(2,1)S(1)}, u32[]{:S(2)}, u32[]{:S(2)}) collective-permute-start(bf16[16,1792]{1,0:T(8,128)(2,1)S(1)} %get-tuple-element.40), channel_id=1, source_target_pairs={{0,8},{4,12},{8,0},{12,4},{1,9},{5,13},{9,1},{13,5},{2,10},{6,14},... | collective-permute-start | bytes 172040 | tf_op jit(solution)/shard_map/ppermute | solution.py:116
  50.2 0.2 collective-permute-start.20
  50.4 0.0 collective-permute-done.18.refs_1_
  50.4 3.4 %collective-permute-done.19.refs_2_ = bf16[16,1792]{1,0:T(8,128)(2,1)S(1)} collective-permute-done((bf16[16,1792]{1,0:T(8,128)(2,1)S(1)}, bf16[16,1792]{1,0:T(8,128)(2,1)S(1)}, u32[]{:S(2)}, u32[]{:S(2)}) %collective-permute-start.19) | collective-permute-done | bytes 57376 | tf_op jit(solution)/shard_map/ppermute | solution.py:116
  53.8 2.4 %collective-permute-done.20.refs_3_ = bf16[16,1792]{1,0:T(8,128)(2,1)S(1)} collective-permute-done((bf16[16,1792]{1,0:T(8,128)(2,1)S(1)}, bf16[16,1792]{1,0:T(8,128)(2,1)S(1)}, u32[]{:S(2)}, u32[]{:S(2)}) %collective-permute-start.20) | collective-permute-done | bytes 57376 | tf_op jit(solution)/shard_map/ppermute | solution.py:116
  56.2 0.7 %shard_map.101 = (bf16[64,1536]{1,0:T(8,128)(2,1)}, f32[7,2,15]{2,1,0:T(2,128)}) custom-call(bf16[16,1792]{1,0:T(8,128)(2,1)S(1)} %get-tuple-element.38.refs_0_, bf16[16,1792]{1,0:T(8,128)(2,1)S(1)} %collective-permute-done.18.refs_1_, bf16[16,1792]{1,0:T(8,128)(2,1)S(1)} %collective-permute-done.19.refs_2_, bf16[16,1792]{1,0:T(8,128)(2,1)S(1)} %collective-permute-done.20.refs_3_), custom_call_target="tpu_custom_call" | custom-call | tf_op jit(solution)/shard_map/pallas_call | solution.py:441
  (3 shorter events, 0.0 us)
Async XLA Ops:
  0.6 24.1 %collective-permute-start.9 = (bf16[1152,1536]{1,0:T(8,128)(2,1)}, bf16[1152,1536]{1,0:T(8,128)(2,1)S(1)}, u32[]{:S(2)}, u32[]{:S(2)}) collective-permute-start(bf16[1152,1536]{1,0:T(8,128)(2,1)} %bitcast.7), channel_id=1, source_target_pairs={{0,1},{1,0},{2,3},{3,2},{4,5},{5,4},{6,7},{7,6},{8,9},{9,8},{10,11... | collective-permute-start | bytes 10616840 | tf_op jit(solution)/shard_map/ppermute | solution.py:116
  1.2 23.5 %collective-permute-start.10 = (bf16[384,1536]{1,0:T(8,128)(2,1)}, bf16[384,1536]{1,0:T(8,128)(2,1)S(1)}, u32[]{:S(2)}, u32[]{:S(2)}) collective-permute-start(bf16[384,1536]{1,0:T(8,128)(2,1)} %refs_11_.2), channel_id=1, source_target_pairs={{0,1},{1,0},{2,3},{3,2},{4,5},{5,4},{6,7},{7,6},{8,9},{9,8},{10,11... | collective-permute-start | bytes 3538952 | tf_op jit(solution)/shard_map/ppermute | solution.py:116
  1.3 30.0 %collective-permute-start.12 = (bf16[2,1536,256]{2,1,0:T(8,128)(2,1)}, bf16[2,1536,256]{2,1,0:T(8,128)(2,1)S(1)}, u32[]{:S(2)}, u32[]{:S(2)}) collective-permute-start(bf16[2,1536,256]{2,1,0:T(8,128)(2,1)} %refs_11_.3), channel_id=1, source_target_pairs={{0,1},{1,0},{2,3},{3,2},{4,5},{5,4},{6,7},{7,6},{8,9},{9,8},{10,11... | collective-permute-start | bytes 4718600 | tf_op jit(solution)/shard_map/ppermute | solution.py:116
  2.7 5.2 %collective-permute-start.1 = (bf16[16,1536]{1,0:T(8,128)(2,1)S(1)}, bf16[16,1536]{1,0:T(8,128)(2,1)S(1)}, u32[]{:S(2)}, u32[]{:S(2)}) collective-permute-start(bf16[16,1536]{1,0:T(8,128)(2,1)S(1)} %get-tuple-element.26), channel_id=1, source_target_pairs={{0,4},{4,0},{8,12},{12,8},{1,5},{5,1},{9,13},{13,9},{2,6},{6,2},{1... | collective-permute-start | bytes 147464 | tf_op jit(solution)/shard_map/ppermute | solution.py:116
  5.4 5.9 %collective-permute-start.2 = (bf16[16,1536]{1,0:T(8,128)(2,1)S(1)}, bf16[16,1536]{1,0:T(8,128)(2,1)S(1)}, u32[]{:S(2)}, u32[]{:S(2)}) collective-permute-start(bf16[16,1536]{1,0:T(8,128)(2,1)S(1)} %get-tuple-element.27), channel_id=1, source_target_pairs={{0,12},{4,8},{8,4},{12,0},{1,13},{5,9},{9,5},{13,1},{2,14},{6,10},... | collective-permute-start | bytes 147464 | tf_op jit(solution)/shard_map/ppermute | solution.py:116
  7.8 5.0 %collective-permute-start = (bf16[16,1536]{1,0:T(8,128)(2,1)S(1)}, bf16[16,1536]{1,0:T(8,128)(2,1)S(1)}, u32[]{:S(2)}, u32[]{:S(2)}) collective-permute-start(bf16[16,1536]{1,0:T(8,128)(2,1)S(1)} %get-tuple-element.24), channel_id=1, source_target_pairs={{0,8},{4,12},{8,0},{12,4},{1,9},{5,13},{9,1},{13,5},{2,10},{6,14},... | collective-permute-start | bytes 147464 | tf_op jit(solution)/shard_map/ppermute | solution.py:116
  11.3 4.6 %collective-permute-start.6 = (bf16[16,1536]{1,0:T(8,128)(2,1)S(1)}, bf16[16,1536]{1,0:T(8,128)(2,1)S(1)}, u32[]{:S(2)}, u32[]{:S(2)}) collective-permute-start(bf16[16,1536]{1,0:T(8,128)(2,1)S(1)} %get-tuple-element.28.refs_1_), channel_id=1, source_target_pairs={{0,2},{1,3},{2,0},{3,1},{4,6},{5,7},{6,4},{7,5},{8,10},{9,11},{10,... | collective-permute-start | bytes 147464 | tf_op jit(solution)/shard_map/ppermute | solution.py:116
  12.8 4.2 %collective-permute-start.5 = (bf16[16,1536]{1,0:T(8,128)(2,1)S(1)}, bf16[16,1536]{1,0:T(8,128)(2,1)S(1)}, u32[]{:S(2)}, u32[]{:S(2)}) collective-permute-start(bf16[16,1536]{1,0:T(8,128)(2,1)S(1)} %get-tuple-element.25.refs_0_), channel_id=1, source_target_pairs={{0,2},{1,3},{2,0},{3,1},{4,6},{5,7},{6,4},{7,5},{8,10},{9,11},{10,... | collective-permute-start | bytes 147464 | tf_op jit(solution)/shard_map/ppermute | solution.py:116
  15.8 1.6 %collective-permute-start.4 = (bf16[16,1536]{1,0:T(8,128)(2,1)S(1)}, bf16[16,1536]{1,0:T(8,128)(2,1)S(1)}, u32[]{:S(2)}, u32[]{:S(2)}) collective-permute-start(bf16[16,1536]{1,0:T(8,128)(2,1)S(1)} %get-tuple-element.30), channel_id=1, source_target_pairs={{0,1},{1,0},{2,3},{3,2},{4,5},{5,4},{6,7},{7,6},{8,9},{9,8},{10,11... | collective-permute-start | bytes 147464 | tf_op jit(solution)/shard_map/ppermute | solution.py:116
  17.0 4.0 %collective-permute-start.8 = (bf16[16,1536]{1,0:T(8,128)(2,1)S(1)}, bf16[16,1536]{1,0:T(8,128)(2,1)S(1)}, u32[]{:S(2)}, u32[]{:S(2)}) collective-permute-start(bf16[16,1536]{1,0:T(8,128)(2,1)S(1)} %get-tuple-element.30), channel_id=1, source_target_pairs={{0,3},{1,2},{2,1},{3,0},{4,7},{5,6},{6,5},{7,4},{8,11},{9,10},{10,... | collective-permute-start | bytes 147464 | tf_op jit(solution)/shard_map/ppermute | solution.py:116
  17.5 3.8 %collective-permute-start.3 = (bf16[16,1536]{1,0:T(8,128)(2,1)S(1)}, bf16[16,1536]{1,0:T(8,128)(2,1)S(1)}, u32[]{:S(2)}, u32[]{:S(2)}) collective-permute-start(bf16[16,1536]{1,0:T(8,128)(2,1)S(1)} %get-tuple-element.29), channel_id=1, source_target_pairs={{0,1},{1,0},{2,3},{3,2},{4,5},{5,4},{6,7},{7,6},{8,9},{9,8},{10,11... | collective-permute-start | bytes 147464 | tf_op jit(solution)/shard_map/ppermute | solution.py:116
  21.0 3.7 %collective-permute-start.7 = (bf16[16,1536]{1,0:T(8,128)(2,1)S(1)}, bf16[16,1536]{1,0:T(8,128)(2,1)S(1)}, u32[]{:S(2)}, u32[]{:S(2)}) collective-permute-start(bf16[16,1536]{1,0:T(8,128)(2,1)S(1)} %get-tuple-element.29), channel_id=1, source_target_pairs={{0,3},{1,2},{2,1},{3,0},{4,7},{5,6},{6,5},{7,4},{8,11},{9,10},{10,... | collective-permute-start | bytes 147464 | tf_op jit(solution)/shard_map/ppermute | solution.py:116
  24.7 15.4 %copy-start = (bf16[2,1536,256]{2,1,0:T(8,128)(2,1)S(1)}, bf16[2,1536,256]{2,1,0:T(8,128)(2,1)}, u32[]{:S(2)}) copy-start(bf16[2,1536,256]{2,1,0:T(8,128)(2,1)} %refs_11_.3) | copy-start | bytes 4718596
  28.8 11.2 %collective-permute-start.11 = (bf16[128,1536]{1,0:T(8,128)(2,1)S(1)}, bf16[128,1536]{1,0:T(8,128)(2,1)S(1)}, u32[]{:S(2)}, u32[]{:S(2)}) collective-permute-start(bf16[128,1536]{1,0:T(8,128)(2,1)S(1)} %shard_map.98.refs_8_), channel_id=1, source_target_pairs={{0,2},{2,0},{1,3},{3,1},{4,6},{6,4},{5,7},{7,5},{8,10},{10,8},{9,1... | collective-permute-start | bytes 1179656 | tf_op jit(solution)/shard_map/ppermute | solution.py:116
  30.1 1.2 %collective-permute-start.13 = (f32[7,256]{1,0:T(8,128)S(1)}, f32[7,256]{1,0:T(8,128)S(1)}, u32[]{:S(2)}, u32[]{:S(2)}) collective-permute-start(f32[7,256]{1,0:T(8,128)S(1)} %get-tuple-element.33.refs_13_), channel_id=1, source_target_pairs={{0,1},{1,0},{2,3},{3,2},{4,5},{5,4},{6,7},{7,6},{8,9},{9,8},{10,11... | collective-permute-start | bytes 21512 | tf_op jit(solution)/shard_map/ppermute | solution.py:116
  41.3 4.6 %collective-permute-start.14 = (bf16[32,1536]{1,0:T(8,128)(2,1)S(1)}, bf16[32,1536]{1,0:T(8,128)(2,1)S(1)}, u32[]{:S(2)}, u32[]{:S(2)}) collective-permute-start(bf16[32,1536]{1,0:T(8,128)(2,1)S(1)} %get-tuple-element.36), channel_id=1, source_target_pairs={{0,1},{1,0},{2,3},{3,2},{4,5},{5,4},{6,7},{7,6},{8,9},{9,8},{10,11... | collective-permute-start | bytes 294920 | tf_op jit(solution)/shard_map/ppermute | solution.py:116
  41.3 1.9 %collective-permute-start.15 = (f32[16,128]{1,0:T(8,128)S(1)}, f32[16,128]{1,0:T(8,128)S(1)}, u32[]{:S(2)}, u32[]{:S(2)}) collective-permute-start(f32[16,128]{1,0:T(8,128)S(1)} %get-tuple-element.37.refs_0_), channel_id=1, source_target_pairs={{0,1},{1,0},{2,3},{3,2},{4,5},{5,4},{6,7},{7,6},{8,9},{9,8},{10,11... | collective-permute-start | bytes 24584 | tf_op jit(solution)/shard_map/ppermute | solution.py:116
  41.8 3.7 %collective-permute-start.16 = (f32[16,128]{1,0:T(8,128)S(1)}, f32[16,128]{1,0:T(8,128)S(1)}, u32[]{:S(2)}, u32[]{:S(2)}) collective-permute-start(f32[16,128]{1,0:T(8,128)S(1)} %get-tuple-element.37.refs_0_), channel_id=1, source_target_pairs={{0,2},{1,3},{2,0},{3,1},{4,6},{5,7},{6,4},{7,5},{8,10},{9,11},{10,... | collective-permute-start | bytes 24584 | tf_op jit(solution)/shard_map/ppermute | solution.py:116
  42.8 3.1 %collective-permute-start.17 = (f32[16,128]{1,0:T(8,128)S(1)}, f32[16,128]{1,0:T(8,128)S(1)}, u32[]{:S(2)}, u32[]{:S(2)}) collective-permute-start(f32[16,128]{1,0:T(8,128)S(1)} %get-tuple-element.37.refs_0_), channel_id=1, source_target_pairs={{0,3},{1,2},{2,1},{3,0},{4,7},{5,6},{6,5},{7,4},{8,11},{9,10},{10,... | collective-permute-start | bytes 24584 | tf_op jit(solution)/shard_map/ppermute | solution.py:116
  46.0 4.5 %collective-permute-start.18 = (bf16[16,1792]{1,0:T(8,128)(2,1)S(1)}, bf16[16,1792]{1,0:T(8,128)(2,1)S(1)}, u32[]{:S(2)}, u32[]{:S(2)}) collective-permute-start(bf16[16,1792]{1,0:T(8,128)(2,1)S(1)} %get-tuple-element.39), channel_id=1, source_target_pairs={{0,4},{4,0},{8,12},{12,8},{1,5},{5,1},{9,13},{13,9},{2,6},{6,2},{1... | collective-permute-start | bytes 172040 | tf_op jit(solution)/shard_map/ppermute | solution.py:116
  47.2 6.6 %collective-permute-start.19 = (bf16[16,1792]{1,0:T(8,128)(2,1)S(1)}, bf16[16,1792]{1,0:T(8,128)(2,1)S(1)}, u32[]{:S(2)}, u32[]{:S(2)}) collective-permute-start(bf16[16,1792]{1,0:T(8,128)(2,1)S(1)} %get-tuple-element.40), channel_id=1, source_target_pairs={{0,8},{4,12},{8,0},{12,4},{1,9},{5,13},{9,1},{13,5},{2,10},{6,14},... | collective-permute-start | bytes 172040 | tf_op jit(solution)/shard_map/ppermute | solution.py:116
  50.2 6.0 %collective-permute-start.20 = (bf16[16,1792]{1,0:T(8,128)(2,1)S(1)}, bf16[16,1792]{1,0:T(8,128)(2,1)S(1)}, u32[]{:S(2)}, u32[]{:S(2)}) collective-permute-start(bf16[16,1792]{1,0:T(8,128)(2,1)S(1)} %get-tuple-element.41), channel_id=1, source_target_pairs={{0,12},{4,8},{8,4},{12,0},{1,13},{5,9},{9,5},{13,1},{2,14},{6,10},... | collective-permute-start | bytes 172040 | tf_op jit(solution)/shard_map/ppermute | solution.py:116

commit v3 on v2

--- a/solution.py
+++ b/solution.py
@@ -162,22 +162,25 @@
     lax.fori_loop(0, count, lambda index, carry: (body(index), carry)[1], 0)
 
 
+def load_kernel(*refs):
+    *refs, sems = refs
+    half = len(refs) // 2
+    copies = [
+        pltpu.make_async_copy(refs[index], refs[half + index], sems.at[index])
+        for index in range(half)
+    ]
+    for copy in copies:
+        copy.start()
+    for copy in copies:
+        copy.wait()
+
+
 def attend_kernel(cols, heads, head_dim, *refs):
-    *token_refs, gain_ref, wq_far, wq_pal, wo_far, wo_pal, out_ref = refs[:-6]
-    normed_ref, qkv_ref, mixed_ref, wq_own, wo_own, sems = refs[-6:]
+    *token_refs, gain_ref, wq_own, wq_pal, wo_own, wo_pal, out_ref = refs[:-3]
+    normed_ref, qkv_ref, mixed_ref = refs[-3:]
     triple = 3 * head_dim
     inner = heads * head_dim
     group = 2 if heads % 2 == 0 else 1
-    chunk = group * triple
-
-    def fetch(index):
-        piece = pl.ds(aligned(index * chunk, chunk), chunk)
-        return pltpu.make_async_copy(wq_far.at[piece, :], wq_own.at[piece, :], sems.at[index])
-
-    for index in range(heads // group):
-        fetch(index).start()
-    fetch_out = pltpu.make_async_copy(wo_far, wo_own, sems.at[heads // group])
-    fetch_out.start()
     gain_row = lined(gain_ref)
     first = 0
     for ref in token_refs:
@@ -195,15 +198,11 @@
 
     large = heads * triple // group
 
-    def project_pal(index):
+    def project_both(index):
         project(wq_pal, index * large, large, index * large)
-
-    def project_own(index):
-        fetch(index).wait()
-        project(wq_own, index * chunk, chunk, heads * triple + index * chunk)
-
-    each(group, project_pal)
-    each(heads // group, project_own)
+        project(wq_own, index * large, large, heads * triple + index * large)
+
+    each(group, project_both)
     left = lax.broadcasted_iota(jnp.int32, (rows, rows), 0) % cols
     right = lax.broadcasted_iota(jnp.int32, (rows, rows), 1) % cols
     same = left == right
@@ -221,7 +220,6 @@
         mixed_ref[head * head_dim : (head + 1) * head_dim, :] = jnp.dot(
             val, weights.astype(jnp.bfloat16), preferred_element_type=jnp.float32
         ).astype(jnp.bfloat16)
-    fetch_out.wait()
     total = None
     for index, wo_ref in enumerate((wo_pal, wo_own)):
         product = lax.dot_general(
@@ -301,8 +299,9 @@
     low = (total - high.astype(jnp.float32)).astype(jnp.bfloat16)
     height, lanes = total.shape
     for block_ref in block_refs:
-        block_ref[:height, width : width + lanes] = high
-        block_ref[:height, width + lanes :] = low
+        block_ref[:height, width:] = jnp.concatenate(
+            [high[:, : lanes // 2], low[:, : lanes // 2]], axis=1
+        )
     for lower, (first_ref, second_ref) in enumerate(
         ((arrived_ref, kept_ref), (kept_ref, arrived_ref))
     ):
@@ -319,15 +318,15 @@
 def place_kernel(seq_count, wide, *refs):
     block_refs, (hidden_ref, actions_ref) = refs[:seq_count], refs[seq_count:]
     width = hidden_ref.shape[1]
-    lanes = (block_refs[0].shape[1] - width) // 2
+    lanes = block_refs[0].shape[1] - width
     height = ROLLS * LINES
     total = None
     for step, ref in enumerate(block_refs):
         first = pl.multiple_of((lax.axis_index("seq") ^ step) * wide, wide)
         hidden_ref[pl.ds(first, wide), :] = ref[:, :width]
-        part = ref[:height, width : width + lanes].astype(jnp.float32)
-        part = part + ref[:height, width + lanes :].astype(jnp.float32)
+        part = ref[:height, width:].astype(jnp.float32)
         total = part if total is None else total + part
+    total = total[:, : lanes // 2] + total[:, lanes // 2 :]
     outs, _, each = actions_ref.shape
     for roll in range(ROLLS):
         actions_ref[:, roll, :] = total[roll * LINES : roll * LINES + outs, :each]
@@ -386,23 +385,28 @@
             batch.append(swap(pals if step & 1 else mine, ("head", "sub"), step))
         batches.append(batch)
     tokens = [batch[step] for step in range(split_count) for batch in batches]
+    wq_near, wo_near = pl.pallas_call(
+        load_kernel,
+        compiler_params=GRANT,
+        in_specs=[hbm] * 2,
+        out_specs=[vmem] * 2,
+        out_shape=[pltpu.VMEM(value.shape, value.dtype) for value in (wq_own, w_out)],
+        scratch_shapes=[pltpu.SemaphoreType.DMA((2,))],
+    )(off_chip(wq_own), off_chip(w_out))
     rows = split_count * seq_count * cols
     inner = heads * head_dim
     branch = pl.pallas_call(
         functools.partial(attend_kernel, cols, heads, head_dim),
         compiler_params=GRANT,
-        in_specs=[vmem] * (2 * split_count + 1) + [hbm, vmem, hbm, vmem],
+        in_specs=[vmem] * (2 * split_count + 5),
         out_specs=vmem,
         out_shape=pltpu.VMEM((rows, width), jnp.bfloat16),
         scratch_shapes=[
             pltpu.VMEM((rows, width), jnp.bfloat16),
             pltpu.VMEM((6 * inner, rows), jnp.bfloat16),
             pltpu.VMEM((2 * inner, rows), jnp.bfloat16),
-            pltpu.VMEM((3 * inner, width), jnp.bfloat16),
-            pltpu.VMEM((inner, width), jnp.bfloat16),
-            pltpu.SemaphoreType.DMA((heads + 1,)),
         ],
-    )(*tokens, attn_gain, off_chip(wq_own), wq_pal, off_chip(w_out), wo_pal)
+    )(*tokens, attn_gain, wq_near, wq_pal, wo_near, wo_pal)
     others = [swap(branch, "head", step) for step in range(1, head_count)]
     embed = w_pair.shape[2]
     wanted = pair_frames.shape[1]
@@ -432,7 +436,7 @@
         compiler_params=GRANT,
         in_specs=[vmem] * (2 + split_count),
         out_specs=[vmem] * seq_count,
-        out_shape=[pltpu.VMEM((wide, width + 256), jnp.bfloat16)] * seq_count,
+        out_shape=[pltpu.VMEM((wide, width + 128), jnp.bfloat16)] * seq_count,
     )(kept, arrived, *parts)
     cut_blocks = blocks
     blocks = [cut_blocks[0]]
@@ -458,7 +462,7 @@
     one_frame = seq_count * head_count * lax.axis_size("sub") == F
     tiled = rows_own % (seq_count * 16) == 0 and lax.axis_size("sub") == 2
     tiled = tiled and rows_own // seq_count >= ROLLS * LINES
-    tiled = tiled and pair_frames.shape[1] <= 128 and w_act.shape[1] <= LINES
+    tiled = tiled and pair_frames.shape[1] <= 64 and w_act.shape[1] <= LINES
     tiled = tiled and frames_in.shape[1] % 128 == 0
     chosen = fast_shards if powers and one_frame and tiled else general_shards
     return chosen(frames_in, attn_gain, w_qkv, w_out, vit_gain, w_pair, w_act, pair_frames)

time: 57.1 us -> 56.6 us (level)
  waiting for transfers between devices: 27.5 us -> 25.3 us
  Pallas kernels: 7.03 us -> 8.81 us
    pallas_call x0 -> x1, Pallas kernels: none -> 2.35 us  [fast_shards(): pl.pallas_call(load_kernel, compiler_params=GRANT, in_specs=[hbm] * 2, ou...]
    ppermute x21, waiting for transfers between devices: 27.5 us -> 25.3 us  [swap(): return on_chip(lax.ppermute(value, axis, pairs))]
    pallas_call x1, Pallas kernels: 4.11 us -> 3.47 us  [fast_shards(): pl.pallas_call(functools.partial(attend_kernel, cols, heads, head_dim), c...]
  transfers between devices with their start and end apart: 21 -> 21, of which waited for: 11 -> 11; matrix products, arithmetic and copies ran while one was open for 0% -> 0% of each run, Pallas kernels for 9% -> 12%
where the time goes in v3:
time: 56.6 us; the launch traced here: 56.4 us
  waiting for transfers between devices  25.3 us (45%)
  starting transfers between devices  21.7 us (38%)
  Pallas kernels  8.81 us (16%)
  between operations  0.69 us (1%)
    ppermute x21, waiting for transfers between devices, swap(): return on_chip(lax.ppermute(value, axis, pairs))  25.3 us
    ppermute x21, starting transfers between devices, swap(): return on_chip(lax.ppermute(value, axis, pairs))  21.7 us
    pallas_call x1, Pallas kernels, fast_shards(): pl.pallas_call(functools.partial(attend_kernel, cols, heads, head_dim), c...  3.47 us
    pallas_call x1, Pallas kernels, fast_shards(): pl.pallas_call(load_kernel, compiler_params=GRANT, in_specs=[hbm] * 2, ou...  2.35 us
    pallas_call x1, Pallas kernels, fast_shards(): pl.pallas_call(functools.partial(pair_kernel, cols, F, order, split_count...  1.23 us
  transfers between devices with their start and end apart: 21, of which 11 were waited for; matrix products, arithmetic and copies ran while one was open for 0% of the time, Pallas kernels for 12%

profile of v3, /device:TPU:0, one launch (start us, length us, event | category | flops | bytes accessed | tf_op | source)
XLA Modules:
  0.0 56.4 jit_solution(3522051532709521955)
XLA Ops:
  0.6 0.6 collective-permute-start.9
  1.2 0.1 collective-permute-start.10
  1.3 0.4 collective-permute-start.12
  1.7 0.9 %shard_map.95 = (bf16[16,1536]{1,0:T(8,128)(2,1)S(1)}, bf16[16,1536]{1,0:T(8,128)(2,1)S(1)}, bf16[16,1536]{1,0:T(8,128)(2,1)S(1)}, bf16[16,1536]{1,0:T(8,128)(2,...) custom-call(bf16[64,1536]{1,0:T(8,128)(2,1)} %tokens_ref.1, ...), custom_call_target="tpu_custom_call" | custom-call | tf_op jit(solution)/shard_map/pallas_call | solution.py:350
  2.7 2.7 %collective-permute-start.1 = (bf16[16,1536]{1,0:T(8,128)(2,1)S(1)}, bf16[16,1536]{1,0:T(8,128)(2,1)S(1)}, u32[]{:S(2)}, u32[]{:S(2)}) collective-permute-start(bf16[16,1536]{1,0:T(8,128)(2,1)S(1)} %get-tuple-element.28), channel_id=1, source_target_pairs={{0,4},{4,0},{8,12},{12,8},{1,5},{5,1},{9,13},{13,9},{2,6},{6,2},{1... | collective-permute-start | bytes 147464 | tf_op jit(solution)/shard_map/ppermute | solution.py:116
  5.4 2.5 %collective-permute-start.2 = (bf16[16,1536]{1,0:T(8,128)(2,1)S(1)}, bf16[16,1536]{1,0:T(8,128)(2,1)S(1)}, u32[]{:S(2)}, u32[]{:S(2)}) collective-permute-start(bf16[16,1536]{1,0:T(8,128)(2,1)S(1)} %get-tuple-element.29), channel_id=1, source_target_pairs={{0,12},{4,8},{8,4},{12,0},{1,13},{5,9},{9,5},{13,1},{2,14},{6,10},... | collective-permute-start | bytes 147464 | tf_op jit(solution)/shard_map/ppermute | solution.py:116
  7.8 0.0 collective-permute-done.1.refs_0_
  7.8 2.6 %collective-permute-start = (bf16[16,1536]{1,0:T(8,128)(2,1)S(1)}, bf16[16,1536]{1,0:T(8,128)(2,1)S(1)}, u32[]{:S(2)}, u32[]{:S(2)}) collective-permute-start(bf16[16,1536]{1,0:T(8,128)(2,1)S(1)} %get-tuple-element.26), channel_id=1, source_target_pairs={{0,8},{4,12},{8,0},{12,4},{1,9},{5,13},{9,1},{13,5},{2,10},{6,14},... | collective-permute-start | bytes 147464 | tf_op jit(solution)/shard_map/ppermute | solution.py:116
  10.5 0.8 %collective-permute-done.2.refs_1_ = bf16[16,1536]{1,0:T(8,128)(2,1)S(1)} collective-permute-done((bf16[16,1536]{1,0:T(8,128)(2,1)S(1)}, bf16[16,1536]{1,0:T(8,128)(2,1)S(1)}, u32[]{:S(2)}, u32[]{:S(2)}) %collective-permute-start.2) | collective-permute-done | bytes 49184 | tf_op jit(solution)/shard_map/ppermute | solution.py:116
  11.3 1.6 %collective-permute-start.6 = (bf16[16,1536]{1,0:T(8,128)(2,1)S(1)}, bf16[16,1536]{1,0:T(8,128)(2,1)S(1)}, u32[]{:S(2)}, u32[]{:S(2)}) collective-permute-start(bf16[16,1536]{1,0:T(8,128)(2,1)S(1)} %get-tuple-element.30.refs_1_), channel_id=1, source_target_pairs={{0,2},{1,3},{2,0},{3,1},{4,6},{5,7},{6,4},{7,5},{8,10},{9,11},{10,... | collective-permute-start | bytes 147464 | tf_op jit(solution)/shard_map/ppermute | solution.py:116
  12.8 0.0 collective-permute-done.refs_1_
  12.8 1.6 %collective-permute-start.5 = (bf16[16,1536]{1,0:T(8,128)(2,1)S(1)}, bf16[16,1536]{1,0:T(8,128)(2,1)S(1)}, u32[]{:S(2)}, u32[]{:S(2)}) collective-permute-start(bf16[16,1536]{1,0:T(8,128)(2,1)S(1)} %get-tuple-element.27.refs_0_), channel_id=1, source_target_pairs={{0,2},{1,3},{2,0},{3,1},{4,6},{5,7},{6,4},{7,5},{8,10},{9,11},{10,... | collective-permute-start | bytes 147464 | tf_op jit(solution)/shard_map/ppermute | solution.py:116
  14.4 1.4 %collective-permute-done.6.refs_5_ = bf16[16,1536]{1,0:T(8,128)(2,1)S(1)} collective-permute-done((bf16[16,1536]{1,0:T(8,128)(2,1)S(1)}, bf16[16,1536]{1,0:T(8,128)(2,1)S(1)}, u32[]{:S(2)}, u32[]{:S(2)}) %collective-permute-start.6) | collective-permute-done | bytes 49184 | tf_op jit(solution)/shard_map/ppermute | solution.py:116
  15.8 0.0 collective-permute-start.4
  15.8 1.1 %collective-permute-done.5.refs_4_ = bf16[16,1536]{1,0:T(8,128)(2,1)S(1)} collective-permute-done((bf16[16,1536]{1,0:T(8,128)(2,1)S(1)}, bf16[16,1536]{1,0:T(8,128)(2,1)S(1)}, u32[]{:S(2)}, u32[]{:S(2)}) %collective-permute-start.5) | collective-permute-done | bytes 49184 | tf_op jit(solution)/shard_map/ppermute | solution.py:116
  17.0 0.5 collective-permute-start.8
  17.5 0.0 collective-permute-done.4.refs_3_
  17.5 1.2 %collective-permute-start.3 = (bf16[16,1536]{1,0:T(8,128)(2,1)S(1)}, bf16[16,1536]{1,0:T(8,128)(2,1)S(1)}, u32[]{:S(2)}, u32[]{:S(2)}) collective-permute-start(bf16[16,1536]{1,0:T(8,128)(2,1)S(1)} %get-tuple-element.31), channel_id=1, source_target_pairs={{0,1},{1,0},{2,3},{3,2},{4,5},{5,4},{6,7},{7,6},{8,9},{9,8},{10,11... | collective-permute-start | bytes 147464 | tf_op jit(solution)/shard_map/ppermute | solution.py:116
  18.6 2.3 %collective-permute-done.8.refs_7_ = bf16[16,1536]{1,0:T(8,128)(2,1)S(1)} collective-permute-done((bf16[16,1536]{1,0:T(8,128)(2,1)S(1)}, bf16[16,1536]{1,0:T(8,128)(2,1)S(1)}, u32[]{:S(2)}, u32[]{:S(2)}) %collective-permute-start.8) | collective-permute-done | bytes 49184 | tf_op jit(solution)/shard_map/ppermute | solution.py:116
  21.0 0.3 collective-permute-start.7
  21.3 2.4 %shard_map.98 = (bf16[1152,1536]{1,0:T(8,128)(2,1)S(1)}, bf16[384,1536]{1,0:T(8,128)(2,1)S(1)}) custom-call(bf16[1152,1536]{1,0:T(8,128)(2,1)} %bitcast.8, bf16[384,1536]{1,0:T(8,128)(2,1)} %refs_1_.1), custom_call_target="tpu_custom_call" | custom-call | tf_op jit(solution)/shard_map/pallas_call | solution.py:388
  23.7 0.0 collective-permute-done.3.refs_2_
  23.7 1.0 %collective-permute-done.7.refs_6_ = bf16[16,1536]{1,0:T(8,128)(2,1)S(1)} collective-permute-done((bf16[16,1536]{1,0:T(8,128)(2,1)S(1)}, bf16[16,1536]{1,0:T(8,128)(2,1)S(1)}, u32[]{:S(2)}, u32[]{:S(2)}) %collective-permute-start.7) | collective-permute-done | bytes 49184 | tf_op jit(solution)/shard_map/ppermute | solution.py:116
  24.7 0.0 collective-permute-done.10.refs_12_
  24.7 0.0 collective-permute-done.9.refs_10_
  24.7 0.0 copy-start
  24.7 3.5 %shard_map.99.refs_8_ = bf16[128,1536]{1,0:T(8,128)(2,1)S(1)} custom-call(bf16[16,1536]{1,0:T(8,128)(2,1)S(1)} %get-tuple-element.27.refs_0_, bf16[16,1536]{1,0:T(8,128)(2,1)S(1)} %get-tuple-element.30.refs_1_, bf16[16,1536]{1,0:T(8,128)(2,1)S(1)} %collective-permute-done.3.refs_2_, bf16[16,1536]{1,0:T(8,128)(2,1)S(1)} %collective-permute-done.4.refs_3_, ...), custom_call_target="tpu_custom_call" | custom-call | tf_op jit(solution)/shard_map/pallas_call | solution.py:398
  28.2 1.3 %collective-permute-start.11 = (bf16[128,1536]{1,0:T(8,128)(2,1)S(1)}, bf16[128,1536]{1,0:T(8,128)(2,1)S(1)}, u32[]{:S(2)}, u32[]{:S(2)}) collective-permute-start(bf16[128,1536]{1,0:T(8,128)(2,1)S(1)} %shard_map.99.refs_8_), channel_id=1, source_target_pairs={{0,2},{2,0},{1,3},{3,1},{4,6},{6,4},{5,7},{7,5},{8,10},{10,8},{9,1... | collective-permute-start | bytes 1179656 | tf_op jit(solution)/shard_map/ppermute | solution.py:116
  29.5 0.0 collective-permute-start.13
  29.5 1.2 %collective-permute-done.13.refs_14_ = f32[7,256]{1,0:T(8,128)S(1)} collective-permute-done((f32[7,256]{1,0:T(8,128)S(1)}, f32[7,256]{1,0:T(8,128)S(1)}, u32[]{:S(2)}, u32[]{:S(2)}) %collective-permute-start.13) | collective-permute-done | bytes 7200 | tf_op jit(solution)/shard_map/ppermute | solution.py:116
  30.6 0.0 collective-permute-done.12.refs_12_
  30.6 8.7 %collective-permute-done.11.refs_9_ = bf16[128,1536]{1,0:T(8,128)(2,1)S(1)} collective-permute-done((bf16[128,1536]{1,0:T(8,128)(2,1)S(1)}, bf16[128,1536]{1,0:T(8,128)(2,1)S(1)}, u32[]{:S(2)}, u32[]{:S(2)}) %collective-permute-start.11) | collective-permute-done | bytes 393248 | tf_op jit(solution)/shard_map/ppermute | solution.py:116
  39.4 0.0 copy-done
  39.4 1.2 %shard_map.100 = (bf16[32,1536]{1,0:T(8,128)(2,1)S(1)}, bf16[32,1536]{1,0:T(8,128)(2,1)S(1)}, f32[16,128]{1,0:T(8,128)S(1)}) custom-call(bf16[16,1536]{1,0:T(8,128)(2,1)S(1)} %get-tuple-element.27.refs_0_, bf16[16,1536]{1,0:T(8,128)(2,1)S(1)} %get-tuple-element.30.refs_1_, bf16[16,1536]{1,0:T(8,128)(2,1)S(1)} %collective-permute-done.3.refs_2_, ...), custom_call_target="tpu_custom_call" | custom-call | tf_op jit(solution)/shard_map/pallas_call | solution.py:413
  40.6 0.0 collective-permute-start.14
  40.6 0.5 collective-permute-start.15
  41.1 1.0 %collective-permute-start.16 = (f32[16,128]{1,0:T(8,128)S(1)}, f32[16,128]{1,0:T(8,128)S(1)}, u32[]{:S(2)}, u32[]{:S(2)}) collective-permute-start(f32[16,128]{1,0:T(8,128)S(1)} %get-tuple-element.41.refs_0_), channel_id=1, source_target_pairs={{0,2},{1,3},{2,0},{3,1},{4,6},{5,7},{6,4},{7,5},{8,10},{9,11},{10,... | collective-permute-start | bytes 24584 | tf_op jit(solution)/shard_map/ppermute | solution.py:116
  42.2 0.4 collective-permute-start.17
  42.5 0.0 collective-permute-done.15.refs_1_
  42.5 2.3 %collective-permute-done.16.refs_2_ = f32[16,128]{1,0:T(8,128)S(1)} collective-permute-done((f32[16,128]{1,0:T(8,128)S(1)}, f32[16,128]{1,0:T(8,128)S(1)}, u32[]{:S(2)}, u32[]{:S(2)}) %collective-permute-start.16) | collective-permute-done | bytes 8224 | tf_op jit(solution)/shard_map/ppermute | solution.py:116
  44.8 0.5 collective-permute-done.17.refs_3_
  45.3 0.0 collective-permute-done.14.arrived_ref
  45.3 0.1 shard_map.101
  45.4 1.4 %collective-permute-start.18 = (bf16[16,1664]{1,0:T(8,128)(2,1)S(1)}, bf16[16,1664]{1,0:T(8,128)(2,1)S(1)}, u32[]{:S(2)}, u32[]{:S(2)}) collective-permute-start(bf16[16,1664]{1,0:T(8,128)(2,1)S(1)} %get-tuple-element.43), channel_id=1, source_target_pairs={{0,4},{4,0},{8,12},{12,8},{1,5},{5,1},{9,13},{13,9},{2,6},{6,2},{1... | collective-permute-start | bytes 159752 | tf_op jit(solution)/shard_map/ppermute | solution.py:116
  46.8 3.0 %collective-permute-start.19 = (bf16[16,1664]{1,0:T(8,128)(2,1)S(1)}, bf16[16,1664]{1,0:T(8,128)(2,1)S(1)}, u32[]{:S(2)}, u32[]{:S(2)}) collective-permute-start(bf16[16,1664]{1,0:T(8,128)(2,1)S(1)} %get-tuple-element.44), channel_id=1, source_target_pairs={{0,8},{4,12},{8,0},{12,4},{1,9},{5,13},{9,1},{13,5},{2,10},{6,14},... | collective-permute-start | bytes 159752 | tf_op jit(solution)/shard_map/ppermute | solution.py:116
  49.8 0.0 collective-permute-start.20
  49.8 0.0 collective-permute-done.18.refs_1_
  49.8 3.3 %collective-permute-done.19.refs_2_ = bf16[16,1664]{1,0:T(8,128)(2,1)S(1)} collective-permute-done((bf16[16,1664]{1,0:T(8,128)(2,1)S(1)}, bf16[16,1664]{1,0:T(8,128)(2,1)S(1)}, u32[]{:S(2)}, u32[]{:S(2)}) %collective-permute-start.19) | collective-permute-done | bytes 53280 | tf_op jit(solution)/shard_map/ppermute | solution.py:116
  53.1 2.6 %collective-permute-done.20.refs_3_ = bf16[16,1664]{1,0:T(8,128)(2,1)S(1)} collective-permute-done((bf16[16,1664]{1,0:T(8,128)(2,1)S(1)}, bf16[16,1664]{1,0:T(8,128)(2,1)S(1)}, u32[]{:S(2)}, u32[]{:S(2)}) %collective-permute-start.20) | collective-permute-done | bytes 53280 | tf_op jit(solution)/shard_map/ppermute | solution.py:116
  55.7 0.7 %shard_map.102 = (bf16[64,1536]{1,0:T(8,128)(2,1)}, f32[7,2,15]{2,1,0:T(2,128)}) custom-call(bf16[16,1664]{1,0:T(8,128)(2,1)S(1)} %get-tuple-element.42.refs_0_, bf16[16,1664]{1,0:T(8,128)(2,1)S(1)} %collective-permute-done.18.refs_1_, bf16[16,1664]{1,0:T(8,128)(2,1)S(1)} %collective-permute-done.19.refs_2_, bf16[16,1664]{1,0:T(8,128)(2,1)S(1)} %collective-permute-done.20.refs_3_), custom_call_target="tpu_custom_call" | custom-call | tf_op jit(solution)/shard_map/pallas_call | solution.py:445
  (2 shorter events, 0.0 us)
Async XLA Ops:
  0.6 24.1 %collective-permute-start.9 = (bf16[1152,1536]{1,0:T(8,128)(2,1)}, bf16[1152,1536]{1,0:T(8,128)(2,1)S(1)}, u32[]{:S(2)}, u32[]{:S(2)}) collective-permute-start(bf16[1152,1536]{1,0:T(8,128)(2,1)} %bitcast.7), channel_id=1, source_target_pairs={{0,1},{1,0},{2,3},{3,2},{4,5},{5,4},{6,7},{7,6},{8,9},{9,8},{10,11... | collective-permute-start | bytes 10616840 | tf_op jit(solution)/shard_map/ppermute | solution.py:116
  1.2 23.5 %collective-permute-start.10 = (bf16[384,1536]{1,0:T(8,128)(2,1)}, bf16[384,1536]{1,0:T(8,128)(2,1)S(1)}, u32[]{:S(2)}, u32[]{:S(2)}) collective-permute-start(bf16[384,1536]{1,0:T(8,128)(2,1)} %refs_1_.1), channel_id=1, source_target_pairs={{0,1},{1,0},{2,3},{3,2},{4,5},{5,4},{6,7},{7,6},{8,9},{9,8},{10,11... | collective-permute-start | bytes 3538952 | tf_op jit(solution)/shard_map/ppermute | solution.py:116
  1.3 29.4 %collective-permute-start.12 = (bf16[2,1536,256]{2,1,0:T(8,128)(2,1)}, bf16[2,1536,256]{2,1,0:T(8,128)(2,1)S(1)}, u32[]{:S(2)}, u32[]{:S(2)}) collective-permute-start(bf16[2,1536,256]{2,1,0:T(8,128)(2,1)} %refs_11_.1), channel_id=1, source_target_pairs={{0,1},{1,0},{2,3},{3,2},{4,5},{5,4},{6,7},{7,6},{8,9},{9,8},{10,11... | collective-permute-start | bytes 4718600 | tf_op jit(solution)/shard_map/ppermute | solution.py:116
  2.7 5.2 %collective-permute-start.1 = (bf16[16,1536]{1,0:T(8,128)(2,1)S(1)}, bf16[16,1536]{1,0:T(8,128)(2,1)S(1)}, u32[]{:S(2)}, u32[]{:S(2)}) collective-permute-start(bf16[16,1536]{1,0:T(8,128)(2,1)S(1)} %get-tuple-element.28), channel_id=1, source_target_pairs={{0,4},{4,0},{8,12},{12,8},{1,5},{5,1},{9,13},{13,9},{2,6},{6,2},{1... | collective-permute-start | bytes 147464 | tf_op jit(solution)/shard_map/ppermute | solution.py:116
  5.4 5.9 %collective-permute-start.2 = (bf16[16,1536]{1,0:T(8,128)(2,1)S(1)}, bf16[16,1536]{1,0:T(8,128)(2,1)S(1)}, u32[]{:S(2)}, u32[]{:S(2)}) collective-permute-start(bf16[16,1536]{1,0:T(8,128)(2,1)S(1)} %get-tuple-element.29), channel_id=1, source_target_pairs={{0,12},{4,8},{8,4},{12,0},{1,13},{5,9},{9,5},{13,1},{2,14},{6,10},... | collective-permute-start | bytes 147464 | tf_op jit(solution)/shard_map/ppermute | solution.py:116
  7.8 5.0 %collective-permute-start = (bf16[16,1536]{1,0:T(8,128)(2,1)S(1)}, bf16[16,1536]{1,0:T(8,128)(2,1)S(1)}, u32[]{:S(2)}, u32[]{:S(2)}) collective-permute-start(bf16[16,1536]{1,0:T(8,128)(2,1)S(1)} %get-tuple-element.26), channel_id=1, source_target_pairs={{0,8},{4,12},{8,0},{12,4},{1,9},{5,13},{9,1},{13,5},{2,10},{6,14},... | collective-permute-start | bytes 147464 | tf_op jit(solution)/shard_map/ppermute | solution.py:116
  11.3 4.6 %collective-permute-start.6 = (bf16[16,1536]{1,0:T(8,128)(2,1)S(1)}, bf16[16,1536]{1,0:T(8,128)(2,1)S(1)}, u32[]{:S(2)}, u32[]{:S(2)}) collective-permute-start(bf16[16,1536]{1,0:T(8,128)(2,1)S(1)} %get-tuple-element.30.refs_1_), channel_id=1, source_target_pairs={{0,2},{1,3},{2,0},{3,1},{4,6},{5,7},{6,4},{7,5},{8,10},{9,11},{10,... | collective-permute-start | bytes 147464 | tf_op jit(solution)/shard_map/ppermute | solution.py:116
  12.8 4.2 %collective-permute-start.5 = (bf16[16,1536]{1,0:T(8,128)(2,1)S(1)}, bf16[16,1536]{1,0:T(8,128)(2,1)S(1)}, u32[]{:S(2)}, u32[]{:S(2)}) collective-permute-start(bf16[16,1536]{1,0:T(8,128)(2,1)S(1)} %get-tuple-element.27.refs_0_), channel_id=1, source_target_pairs={{0,2},{1,3},{2,0},{3,1},{4,6},{5,7},{6,4},{7,5},{8,10},{9,11},{10,... | collective-permute-start | bytes 147464 | tf_op jit(solution)/shard_map/ppermute | solution.py:116
  15.8 1.6 %collective-permute-start.4 = (bf16[16,1536]{1,0:T(8,128)(2,1)S(1)}, bf16[16,1536]{1,0:T(8,128)(2,1)S(1)}, u32[]{:S(2)}, u32[]{:S(2)}) collective-permute-start(bf16[16,1536]{1,0:T(8,128)(2,1)S(1)} %get-tuple-element.32), channel_id=1, source_target_pairs={{0,1},{1,0},{2,3},{3,2},{4,5},{5,4},{6,7},{7,6},{8,9},{9,8},{10,11... | collective-permute-start | bytes 147464 | tf_op jit(solution)/shard_map/ppermute | solution.py:116
  17.0 4.0 %collective-permute-start.8 = (bf16[16,1536]{1,0:T(8,128)(2,1)S(1)}, bf16[16,1536]{1,0:T(8,128)(2,1)S(1)}, u32[]{:S(2)}, u32[]{:S(2)}) collective-permute-start(bf16[16,1536]{1,0:T(8,128)(2,1)S(1)} %get-tuple-element.32), channel_id=1, source_target_pairs={{0,3},{1,2},{2,1},{3,0},{4,7},{5,6},{6,5},{7,4},{8,11},{9,10},{10,... | collective-permute-start | bytes 147464 | tf_op jit(solution)/shard_map/ppermute | solution.py:116
  17.5 6.2 %collective-permute-start.3 = (bf16[16,1536]{1,0:T(8,128)(2,1)S(1)}, bf16[16,1536]{1,0:T(8,128)(2,1)S(1)}, u32[]{:S(2)}, u32[]{:S(2)}) collective-permute-start(bf16[16,1536]{1,0:T(8,128)(2,1)S(1)} %get-tuple-element.31), channel_id=1, source_target_pairs={{0,1},{1,0},{2,3},{3,2},{4,5},{5,4},{6,7},{7,6},{8,9},{9,8},{10,11... | collective-permute-start | bytes 147464 | tf_op jit(solution)/shard_map/ppermute | solution.py:116
  21.0 3.7 %collective-permute-start.7 = (bf16[16,1536]{1,0:T(8,128)(2,1)S(1)}, bf16[16,1536]{1,0:T(8,128)(2,1)S(1)}, u32[]{:S(2)}, u32[]{:S(2)}) collective-permute-start(bf16[16,1536]{1,0:T(8,128)(2,1)S(1)} %get-tuple-element.31), channel_id=1, source_target_pairs={{0,3},{1,2},{2,1},{3,0},{4,7},{5,6},{6,5},{7,4},{8,11},{9,10},{10,... | collective-permute-start | bytes 147464 | tf_op jit(solution)/shard_map/ppermute | solution.py:116
  24.7 14.7 %copy-start = (bf16[2,1536,256]{2,1,0:T(8,128)(2,1)S(1)}, bf16[2,1536,256]{2,1,0:T(8,128)(2,1)}, u32[]{:S(2)}) copy-start(bf16[2,1536,256]{2,1,0:T(8,128)(2,1)} %refs_11_.1) | copy-start | bytes 4718596
  28.2 11.2 %collective-permute-start.11 = (bf16[128,1536]{1,0:T(8,128)(2,1)S(1)}, bf16[128,1536]{1,0:T(8,128)(2,1)S(1)}, u32[]{:S(2)}, u32[]{:S(2)}) collective-permute-start(bf16[128,1536]{1,0:T(8,128)(2,1)S(1)} %shard_map.99.refs_8_), channel_id=1, source_target_pairs={{0,2},{2,0},{1,3},{3,1},{4,6},{6,4},{5,7},{7,5},{8,10},{10,8},{9,1... | collective-permute-start | bytes 1179656 | tf_op jit(solution)/shard_map/ppermute | solution.py:116
  29.5 1.2 %collective-permute-start.13 = (f32[7,256]{1,0:T(8,128)S(1)}, f32[7,256]{1,0:T(8,128)S(1)}, u32[]{:S(2)}, u32[]{:S(2)}) collective-permute-start(f32[7,256]{1,0:T(8,128)S(1)} %get-tuple-element.37.refs_13_), channel_id=1, source_target_pairs={{0,1},{1,0},{2,3},{3,2},{4,5},{5,4},{6,7},{7,6},{8,9},{9,8},{10,11... | collective-permute-start | bytes 21512 | tf_op jit(solution)/shard_map/ppermute | solution.py:116
  40.6 4.6 %collective-permute-start.14 = (bf16[32,1536]{1,0:T(8,128)(2,1)S(1)}, bf16[32,1536]{1,0:T(8,128)(2,1)S(1)}, u32[]{:S(2)}, u32[]{:S(2)}) collective-permute-start(bf16[32,1536]{1,0:T(8,128)(2,1)S(1)} %get-tuple-element.40), channel_id=1, source_target_pairs={{0,1},{1,0},{2,3},{3,2},{4,5},{5,4},{6,7},{7,6},{8,9},{9,8},{10,11... | collective-permute-start | bytes 294920 | tf_op jit(solution)/shard_map/ppermute | solution.py:116
  40.6 1.9 %collective-permute-start.15 = (f32[16,128]{1,0:T(8,128)S(1)}, f32[16,128]{1,0:T(8,128)S(1)}, u32[]{:S(2)}, u32[]{:S(2)}) collective-permute-start(f32[16,128]{1,0:T(8,128)S(1)} %get-tuple-element.41.refs_0_), channel_id=1, source_target_pairs={{0,1},{1,0},{2,3},{3,2},{4,5},{5,4},{6,7},{7,6},{8,9},{9,8},{10,11... | collective-permute-start | bytes 24584 | tf_op jit(solution)/shard_map/ppermute | solution.py:116
  41.1 3.7 %collective-permute-start.16 = (f32[16,128]{1,0:T(8,128)S(1)}, f32[16,128]{1,0:T(8,128)S(1)}, u32[]{:S(2)}, u32[]{:S(2)}) collective-permute-start(f32[16,128]{1,0:T(8,128)S(1)} %get-tuple-element.41.refs_0_), channel_id=1, source_target_pairs={{0,2},{1,3},{2,0},{3,1},{4,6},{5,7},{6,4},{7,5},{8,10},{9,11},{10,... | collective-permute-start | bytes 24584 | tf_op jit(solution)/shard_map/ppermute | solution.py:116
  42.2 3.1 %collective-permute-start.17 = (f32[16,128]{1,0:T(8,128)S(1)}, f32[16,128]{1,0:T(8,128)S(1)}, u32[]{:S(2)}, u32[]{:S(2)}) collective-permute-start(f32[16,128]{1,0:T(8,128)S(1)} %get-tuple-element.41.refs_0_), channel_id=1, source_target_pairs={{0,3},{1,2},{2,1},{3,0},{4,7},{5,6},{6,5},{7,4},{8,11},{9,10},{10,... | collective-permute-start | bytes 24584 | tf_op jit(solution)/shard_map/ppermute | solution.py:116
  45.4 4.5 %collective-permute-start.18 = (bf16[16,1664]{1,0:T(8,128)(2,1)S(1)}, bf16[16,1664]{1,0:T(8,128)(2,1)S(1)}, u32[]{:S(2)}, u32[]{:S(2)}) collective-permute-start(bf16[16,1664]{1,0:T(8,128)(2,1)S(1)} %get-tuple-element.43), channel_id=1, source_target_pairs={{0,4},{4,0},{8,12},{12,8},{1,5},{5,1},{9,13},{13,9},{2,6},{6,2},{1... | collective-permute-start | bytes 159752 | tf_op jit(solution)/shard_map/ppermute | solution.py:116
  46.8 6.3 %collective-permute-start.19 = (bf16[16,1664]{1,0:T(8,128)(2,1)S(1)}, bf16[16,1664]{1,0:T(8,128)(2,1)S(1)}, u32[]{:S(2)}, u32[]{:S(2)}) collective-permute-start(bf16[16,1664]{1,0:T(8,128)(2,1)S(1)} %get-tuple-element.44), channel_id=1, source_target_pairs={{0,8},{4,12},{8,0},{12,4},{1,9},{5,13},{9,1},{13,5},{2,10},{6,14},... | collective-permute-start | bytes 159752 | tf_op jit(solution)/shard_map/ppermute | solution.py:116
  49.8 5.9 %collective-permute-start.20 = (bf16[16,1664]{1,0:T(8,128)(2,1)S(1)}, bf16[16,1664]{1,0:T(8,128)(2,1)S(1)}, u32[]{:S(2)}, u32[]{:S(2)}) collective-permute-start(bf16[16,1664]{1,0:T(8,128)(2,1)S(1)} %get-tuple-element.45), channel_id=1, source_target_pairs={{0,12},{4,8},{8,4},{12,0},{1,13},{5,9},{9,5},{13,1},{2,14},{6,10},... | collective-permute-start | bytes 159752 | tf_op jit(solution)/shard_map/ppermute | solution.py:116

commit v4 on v3

--- a/solution.py
+++ b/solution.py
@@ -125,17 +125,15 @@
     return (rows * lax.rsqrt(mean_sq + EPS) * gain_row).astype(jnp.bfloat16)
 
 
-def cut_kernel(seq_count, small, tokens_ref, *refs):
-    small_refs, out_refs, sems = refs[:small], refs[small:-1], refs[-1]
+def cut_kernel(tokens_ref, *refs):
+    out_refs, sems = refs[:-1], refs[-1]
     wide = out_refs[0].shape[0]
     place = lax.axis_index("seq")
     copies = []
-    for step, out_ref in enumerate(out_refs[:seq_count]):
+    for step, out_ref in enumerate(out_refs):
         first = pl.multiple_of((place ^ step) * wide, wide)
         source = tokens_ref.at[pl.ds(first, wide), :]
         copies.append(pltpu.make_async_copy(source, out_ref, sems.at[step]))
-    for source, out_ref in zip(small_refs, out_refs[seq_count:]):
-        copies.append(pltpu.make_async_copy(source, out_ref, sems.at[len(copies)]))
     for copy in copies:
         copy.start()
     for copy in copies:
@@ -346,18 +344,14 @@
     hbm = pl.BlockSpec(memory_space=pltpu.HBM)
     wq_own = jnp.transpose(w_qkv, (1, 2, 0)).reshape(heads * triple, width)
     wa_own = w_act.T
-    small = [attn_gain.reshape(-1, 128), vit_gain.reshape(-1, 128), wa_own, pair_frames]
-    cut = pl.pallas_call(
-        functools.partial(cut_kernel, seq_count, len(small)),
-        compiler_params=GRANT,
-        in_specs=[hbm] * (1 + len(small)),
-        out_specs=[vmem] * (seq_count + len(small)),
-        out_shape=[pltpu.VMEM((wide, width), jnp.bfloat16)] * seq_count
-        + [pltpu.VMEM(value.shape, value.dtype) for value in small],
-        scratch_shapes=[pltpu.SemaphoreType.DMA((seq_count + len(small),))],
-    )(off_chip(frames_in), *[off_chip(value) for value in small])
-    pieces = cut[:seq_count]
-    attn_gain, vit_gain, wa_own, pair_frames = cut[seq_count:]
+    pieces = pl.pallas_call(
+        cut_kernel,
+        compiler_params=GRANT,
+        in_specs=[hbm],
+        out_specs=[vmem] * seq_count,
+        out_shape=[pltpu.VMEM((wide, width), jnp.bfloat16)] * seq_count,
+        scratch_shapes=[pltpu.SemaphoreType.DMA((seq_count,))],
+    )(off_chip(frames_in))
     cut_pieces = pieces
     pieces = [cut_pieces[0]]
     for step in range(1, seq_count):
@@ -385,14 +379,17 @@
             batch.append(swap(pals if step & 1 else mine, ("head", "sub"), step))
         batches.append(batch)
     tokens = [batch[step] for step in range(split_count) for batch in batches]
-    wq_near, wo_near = pl.pallas_call(
+    loads = [
+        wq_own, w_out, attn_gain.reshape(-1, 128), vit_gain.reshape(-1, 128), wa_own, pair_frames
+    ]
+    wq_near, wo_near, attn_gain, vit_gain, wa_near, pair_frames = pl.pallas_call(
         load_kernel,
         compiler_params=GRANT,
-        in_specs=[hbm] * 2,
-        out_specs=[vmem] * 2,
-        out_shape=[pltpu.VMEM(value.shape, value.dtype) for value in (wq_own, w_out)],
-        scratch_shapes=[pltpu.SemaphoreType.DMA((2,))],
-    )(off_chip(wq_own), off_chip(w_out))
+        in_specs=[hbm] * len(loads),
+        out_specs=[vmem] * len(loads),
+        out_shape=[pltpu.VMEM(value.shape, value.dtype) for value in loads],
+        scratch_shapes=[pltpu.SemaphoreType.DMA((len(loads),))],
+    )(*[off_chip(value) for value in loads])
     rows = split_count * seq_count * cols
     inner = heads * head_dim
     branch = pl.pallas_call(
@@ -425,7 +422,7 @@
         ],
     )(
         *tokens, branch, *others, vit_gain, on_chip(w_pair), wp_pal,
-        wa_own, wa_pal, pair_frames,
+        wa_near, wa_pal, pair_frames,
     )
     arrived = swap(passed, "sub", 1)
     parts = [part]

time: 56.6 us -> 56.6 us (level)
  no operation moved by 1% of the time
where the time goes in v4:
time: 56.6 us; the launch traced here: 56.4 us
  waiting for transfers between devices  25.2 us (45%)
  starting transfers between devices  21.6 us (38%)
  Pallas kernels  8.81 us (16%)
  between operations  0.7 us (1%)
    ppermute x21, waiting for transfers between devices, swap(): return on_chip(lax.ppermute(value, axis, pairs))  25.2 us
    ppermute x21, starting transfers between devices, swap(): return on_chip(lax.ppermute(value, axis, pairs))  21.6 us
    pallas_call x1, Pallas kernels, fast_shards(): pl.pallas_call(functools.partial(attend_kernel, cols, heads, head_dim), c...  3.47 us
    pallas_call x1, Pallas kernels, fast_shards(): pl.pallas_call(load_kernel, compiler_params=GRANT, in_specs=[hbm] * len(l...  2.39 us
    pallas_call x1, Pallas kernels, fast_shards(): pl.pallas_call(functools.partial(pair_kernel, cols, F, order, split_count...  1.23 us
  transfers between devices with their start and end apart: 21, of which 11 were waited for; matrix products, arithmetic and copies ran while one was open for 0% of the time, Pallas kernels for 12%

profile of v4, /device:TPU:0, one launch (start us, length us, event | category | flops | bytes accessed | tf_op | source)
XLA Modules:
  0.0 56.4 jit_solution(11953276498614382047)
XLA Ops:
  0.6 0.6 collective-permute-start.9
  1.2 0.1 collective-permute-start.10
  1.3 0.4 collective-permute-start.12
  1.7 0.9 %shard_map.95 = (bf16[16,1536]{1,0:T(8,128)(2,1)S(1)}, bf16[16,1536]{1,0:T(8,128)(2,1)S(1)}, bf16[16,1536]{1,0:T(8,128)(2,1)S(1)}, bf16[16,1536]{1,0:T(8,128)(2,1)S(1)}) custom-call(bf16[64,1536]{1,0:T(8,128)(2,1)} %tokens_ref.1), custom_call_target="tpu_custom_call" | custom-call | tf_op jit(solution)/shard_map/pallas_call | solution.py:347
  2.6 2.7 %collective-permute-start.1 = (bf16[16,1536]{1,0:T(8,128)(2,1)S(1)}, bf16[16,1536]{1,0:T(8,128)(2,1)S(1)}, u32[]{:S(2)}, u32[]{:S(2)}) collective-permute-start(bf16[16,1536]{1,0:T(8,128)(2,1)S(1)} %get-tuple-element.28), channel_id=1, source_target_pairs={{0,4},{4,0},{8,12},{12,8},{1,5},{5,1},{9,13},{13,9},{2,6},{6,2},{1... | collective-permute-start | bytes 147464 | tf_op jit(solution)/shard_map/ppermute | solution.py:116
  5.3 2.5 %collective-permute-start.2 = (bf16[16,1536]{1,0:T(8,128)(2,1)S(1)}, bf16[16,1536]{1,0:T(8,128)(2,1)S(1)}, u32[]{:S(2)}, u32[]{:S(2)}) collective-permute-start(bf16[16,1536]{1,0:T(8,128)(2,1)S(1)} %get-tuple-element.29), channel_id=1, source_target_pairs={{0,12},{4,8},{8,4},{12,0},{1,13},{5,9},{9,5},{13,1},{2,14},{6,10},... | collective-permute-start | bytes 147464 | tf_op jit(solution)/shard_map/ppermute | solution.py:116
  7.8 0.0 collective-permute-done.1.refs_0_
  7.8 2.6 %collective-permute-start = (bf16[16,1536]{1,0:T(8,128)(2,1)S(1)}, bf16[16,1536]{1,0:T(8,128)(2,1)S(1)}, u32[]{:S(2)}, u32[]{:S(2)}) collective-permute-start(bf16[16,1536]{1,0:T(8,128)(2,1)S(1)} %get-tuple-element.26), channel_id=1, source_target_pairs={{0,8},{4,12},{8,0},{12,4},{1,9},{5,13},{9,1},{13,5},{2,10},{6,14},... | collective-permute-start | bytes 147464 | tf_op jit(solution)/shard_map/ppermute | solution.py:116
  10.4 0.8 %collective-permute-done.2.refs_1_ = bf16[16,1536]{1,0:T(8,128)(2,1)S(1)} collective-permute-done((bf16[16,1536]{1,0:T(8,128)(2,1)S(1)}, bf16[16,1536]{1,0:T(8,128)(2,1)S(1)}, u32[]{:S(2)}, u32[]{:S(2)}) %collective-permute-start.2) | collective-permute-done | bytes 49184 | tf_op jit(solution)/shard_map/ppermute | solution.py:116
  11.2 1.6 %collective-permute-start.6 = (bf16[16,1536]{1,0:T(8,128)(2,1)S(1)}, bf16[16,1536]{1,0:T(8,128)(2,1)S(1)}, u32[]{:S(2)}, u32[]{:S(2)}) collective-permute-start(bf16[16,1536]{1,0:T(8,128)(2,1)S(1)} %get-tuple-element.30.refs_1_), channel_id=1, source_target_pairs={{0,2},{1,3},{2,0},{3,1},{4,6},{5,7},{6,4},{7,5},{8,10},{9,11},{10,... | collective-permute-start | bytes 147464 | tf_op jit(solution)/shard_map/ppermute | solution.py:116
  12.8 0.0 collective-permute-done.refs_1_
  12.8 1.6 %collective-permute-start.5 = (bf16[16,1536]{1,0:T(8,128)(2,1)S(1)}, bf16[16,1536]{1,0:T(8,128)(2,1)S(1)}, u32[]{:S(2)}, u32[]{:S(2)}) collective-permute-start(bf16[16,1536]{1,0:T(8,128)(2,1)S(1)} %get-tuple-element.27.refs_0_), channel_id=1, source_target_pairs={{0,2},{1,3},{2,0},{3,1},{4,6},{5,7},{6,4},{7,5},{8,10},{9,11},{10,... | collective-permute-start | bytes 147464 | tf_op jit(solution)/shard_map/ppermute | solution.py:116
  14.4 1.4 %collective-permute-done.6.refs_5_ = bf16[16,1536]{1,0:T(8,128)(2,1)S(1)} collective-permute-done((bf16[16,1536]{1,0:T(8,128)(2,1)S(1)}, bf16[16,1536]{1,0:T(8,128)(2,1)S(1)}, u32[]{:S(2)}, u32[]{:S(2)}) %collective-permute-start.6) | collective-permute-done | bytes 49184 | tf_op jit(solution)/shard_map/ppermute | solution.py:116
  15.8 0.0 collective-permute-start.4
  15.8 1.1 %collective-permute-done.5.refs_4_ = bf16[16,1536]{1,0:T(8,128)(2,1)S(1)} collective-permute-done((bf16[16,1536]{1,0:T(8,128)(2,1)S(1)}, bf16[16,1536]{1,0:T(8,128)(2,1)S(1)}, u32[]{:S(2)}, u32[]{:S(2)}) %collective-permute-start.5) | collective-permute-done | bytes 49184 | tf_op jit(solution)/shard_map/ppermute | solution.py:116
  16.9 0.5 collective-permute-start.8
  17.4 0.0 collective-permute-done.4.refs_3_
  17.4 1.2 %collective-permute-start.3 = (bf16[16,1536]{1,0:T(8,128)(2,1)S(1)}, bf16[16,1536]{1,0:T(8,128)(2,1)S(1)}, u32[]{:S(2)}, u32[]{:S(2)}) collective-permute-start(bf16[16,1536]{1,0:T(8,128)(2,1)S(1)} %get-tuple-element.31), channel_id=1, source_target_pairs={{0,1},{1,0},{2,3},{3,2},{4,5},{5,4},{6,7},{7,6},{8,9},{9,8},{10,11... | collective-permute-start | bytes 147464 | tf_op jit(solution)/shard_map/ppermute | solution.py:116
  18.6 2.3 %collective-permute-done.8.refs_7_ = bf16[16,1536]{1,0:T(8,128)(2,1)S(1)} collective-permute-done((bf16[16,1536]{1,0:T(8,128)(2,1)S(1)}, bf16[16,1536]{1,0:T(8,128)(2,1)S(1)}, u32[]{:S(2)}, u32[]{:S(2)}) %collective-permute-start.8) | collective-permute-done | bytes 49184 | tf_op jit(solution)/shard_map/ppermute | solution.py:116
  20.9 0.3 collective-permute-start.7
  21.3 2.4 %shard_map.98 = (bf16[1152,1536]{1,0:T(8,128)(2,1)S(1)}, bf16[384,1536]{1,0:T(8,128)(2,1)S(1)}, f32[12,128]{1,0:T(8,128)S(1)}, f32[12,128]{1,0:T(8,128)S(1)}, f32[7,256]{1,0:T(8,128)S(1)}, /*index=5*/s32[2,15]{1,0:T(2,128)S(1)}) custom-call(bf16[1152,1536]{1,0:T(8,128)(2,1)} %bitcast.8, bf16[384,1536]{1,0:T(8,128)(2,1)} %refs_1_.1, f32[12,128]{1,0:T(8,128)} %bitcast.9, ...), custom_call_target="tpu_custom_call" | custom-call | tf_op jit(solution)/shard_map/pallas_call | solution.py:385
  23.7 0.0 collective-permute-done.3.refs_2_
  23.7 1.0 %collective-permute-done.7.refs_6_ = bf16[16,1536]{1,0:T(8,128)(2,1)S(1)} collective-permute-done((bf16[16,1536]{1,0:T(8,128)(2,1)S(1)}, bf16[16,1536]{1,0:T(8,128)(2,1)S(1)}, u32[]{:S(2)}, u32[]{:S(2)}) %collective-permute-start.7) | collective-permute-done | bytes 49184 | tf_op jit(solution)/shard_map/ppermute | solution.py:116
  24.7 0.0 collective-permute-done.10.refs_12_
  24.7 0.0 collective-permute-done.9.refs_10_
  24.7 0.0 copy-start.1
  24.7 0.0 copy-start
  24.7 3.5 %shard_map.99.refs_8_ = bf16[128,1536]{1,0:T(8,128)(2,1)S(1)} custom-call(bf16[16,1536]{1,0:T(8,128)(2,1)S(1)} %get-tuple-element.27.refs_0_, bf16[16,1536]{1,0:T(8,128)(2,1)S(1)} %get-tuple-element.30.refs_1_, bf16[16,1536]{1,0:T(8,128)(2,1)S(1)} %collective-permute-done.3.refs_2_, bf16[16,1536]{1,0:T(8,128)(2,1)S(1)} %collective-permute-done.4.refs_3_, ...), custom_call_target="tpu_custom_call" | custom-call | tf_op jit(solution)/shard_map/pallas_call | solution.py:395
  28.2 1.3 %collective-permute-start.11 = (bf16[128,1536]{1,0:T(8,128)(2,1)S(1)}, bf16[128,1536]{1,0:T(8,128)(2,1)S(1)}, u32[]{:S(2)}, u32[]{:S(2)}) collective-permute-start(bf16[128,1536]{1,0:T(8,128)(2,1)S(1)} %shard_map.99.refs_8_), channel_id=1, source_target_pairs={{0,2},{2,0},{1,3},{3,1},{4,6},{6,4},{5,7},{7,5},{8,10},{10,8},{9,1... | collective-permute-start | bytes 1179656 | tf_op jit(solution)/shard_map/ppermute | solution.py:116
  29.4 0.0 copy-done.1
  29.4 0.0 collective-permute-start.13
  29.4 1.2 %collective-permute-done.13.refs_14_ = f32[7,256]{1,0:T(8,128)S(1)} collective-permute-done((f32[7,256]{1,0:T(8,128)S(1)}, f32[7,256]{1,0:T(8,128)S(1)}, u32[]{:S(2)}, u32[]{:S(2)}) %collective-permute-start.13) | collective-permute-done | bytes 7200 | tf_op jit(solution)/shard_map/ppermute | solution.py:116
  30.6 0.0 collective-permute-done.12.refs_12_
  30.6 8.7 %collective-permute-done.11.refs_9_ = bf16[128,1536]{1,0:T(8,128)(2,1)S(1)} collective-permute-done((bf16[128,1536]{1,0:T(8,128)(2,1)S(1)}, bf16[128,1536]{1,0:T(8,128)(2,1)S(1)}, u32[]{:S(2)}, u32[]{:S(2)}) %collective-permute-start.11) | collective-permute-done | bytes 393248 | tf_op jit(solution)/shard_map/ppermute | solution.py:116
  39.4 0.0 copy-done
  39.4 1.2 %shard_map.100 = (bf16[32,1536]{1,0:T(8,128)(2,1)S(1)}, bf16[32,1536]{1,0:T(8,128)(2,1)S(1)}, f32[16,128]{1,0:T(8,128)S(1)}) custom-call(bf16[16,1536]{1,0:T(8,128)(2,1)S(1)} %get-tuple-element.27.refs_0_, bf16[16,1536]{1,0:T(8,128)(2,1)S(1)} %get-tuple-element.30.refs_1_, bf16[16,1536]{1,0:T(8,128)(2,1)S(1)} %collective-permute-done.3.refs_2_, ...), custom_call_target="tpu_custom_call" | custom-call | tf_op jit(solution)/shard_map/pallas_call | solution.py:410
  40.6 0.0 collective-permute-start.14
  40.6 0.5 collective-permute-start.15
  41.1 1.0 %collective-permute-start.16 = (f32[16,128]{1,0:T(8,128)S(1)}, f32[16,128]{1,0:T(8,128)S(1)}, u32[]{:S(2)}, u32[]{:S(2)}) collective-permute-start(f32[16,128]{1,0:T(8,128)S(1)} %get-tuple-element.41.refs_0_), channel_id=1, source_target_pairs={{0,2},{1,3},{2,0},{3,1},{4,6},{5,7},{6,4},{7,5},{8,10},{9,11},{10,... | collective-permute-start | bytes 24584 | tf_op jit(solution)/shard_map/ppermute | solution.py:116
  42.1 0.4 collective-permute-start.17
  42.5 0.0 collective-permute-done.15.refs_1_
  42.5 2.3 %collective-permute-done.16.refs_2_ = f32[16,128]{1,0:T(8,128)S(1)} collective-permute-done((f32[16,128]{1,0:T(8,128)S(1)}, f32[16,128]{1,0:T(8,128)S(1)}, u32[]{:S(2)}, u32[]{:S(2)}) %collective-permute-start.16) | collective-permute-done | bytes 8224 | tf_op jit(solution)/shard_map/ppermute | solution.py:116
  44.8 0.4 collective-permute-done.17.refs_3_
  45.2 0.0 collective-permute-done.14.arrived_ref
  45.2 0.1 shard_map.101
  45.3 1.4 %collective-permute-start.18 = (bf16[16,1664]{1,0:T(8,128)(2,1)S(1)}, bf16[16,1664]{1,0:T(8,128)(2,1)S(1)}, u32[]{:S(2)}, u32[]{:S(2)}) collective-permute-start(bf16[16,1664]{1,0:T(8,128)(2,1)S(1)} %get-tuple-element.43), channel_id=1, source_target_pairs={{0,4},{4,0},{8,12},{12,8},{1,5},{5,1},{9,13},{13,9},{2,6},{6,2},{1... | collective-permute-start | bytes 159752 | tf_op jit(solution)/shard_map/ppermute | solution.py:116
  46.8 3.0 %collective-permute-start.19 = (bf16[16,1664]{1,0:T(8,128)(2,1)S(1)}, bf16[16,1664]{1,0:T(8,128)(2,1)S(1)}, u32[]{:S(2)}, u32[]{:S(2)}) collective-permute-start(bf16[16,1664]{1,0:T(8,128)(2,1)S(1)} %get-tuple-element.44), channel_id=1, source_target_pairs={{0,8},{4,12},{8,0},{12,4},{1,9},{5,13},{9,1},{13,5},{2,10},{6,14},... | collective-permute-start | bytes 159752 | tf_op jit(solution)/shard_map/ppermute | solution.py:116
  49.8 0.0 collective-permute-start.20
  49.8 0.0 collective-permute-done.18.refs_1_
  49.8 3.3 %collective-permute-done.19.refs_2_ = bf16[16,1664]{1,0:T(8,128)(2,1)S(1)} collective-permute-done((bf16[16,1664]{1,0:T(8,128)(2,1)S(1)}, bf16[16,1664]{1,0:T(8,128)(2,1)S(1)}, u32[]{:S(2)}, u32[]{:S(2)}) %collective-permute-start.19) | collective-permute-done | bytes 53280 | tf_op jit(solution)/shard_map/ppermute | solution.py:116
  53.1 2.6 %collective-permute-done.20.refs_3_ = bf16[16,1664]{1,0:T(8,128)(2,1)S(1)} collective-permute-done((bf16[16,1664]{1,0:T(8,128)(2,1)S(1)}, bf16[16,1664]{1,0:T(8,128)(2,1)S(1)}, u32[]{:S(2)}, u32[]{:S(2)}) %collective-permute-start.20) | collective-permute-done | bytes 53280 | tf_op jit(solution)/shard_map/ppermute | solution.py:116
  55.7 0.7 %shard_map.102 = (bf16[64,1536]{1,0:T(8,128)(2,1)}, f32[7,2,15]{2,1,0:T(2,128)}) custom-call(bf16[16,1664]{1,0:T(8,128)(2,1)S(1)} %get-tuple-element.42.refs_0_, bf16[16,1664]{1,0:T(8,128)(2,1)S(1)} %collective-permute-done.18.refs_1_, bf16[16,1664]{1,0:T(8,128)(2,1)S(1)} %collective-permute-done.19.refs_2_, bf16[16,1664]{1,0:T(8,128)(2,1)S(1)} %collective-permute-done.20.refs_3_), custom_call_target="tpu_custom_call" | custom-call | tf_op jit(solution)/shard_map/pallas_call | solution.py:442
  (2 shorter events, 0.0 us)
Async XLA Ops:
  0.6 24.0 %collective-permute-start.9 = (bf16[1152,1536]{1,0:T(8,128)(2,1)}, bf16[1152,1536]{1,0:T(8,128)(2,1)S(1)}, u32[]{:S(2)}, u32[]{:S(2)}) collective-permute-start(bf16[1152,1536]{1,0:T(8,128)(2,1)} %bitcast.7), channel_id=1, source_target_pairs={{0,1},{1,0},{2,3},{3,2},{4,5},{5,4},{6,7},{7,6},{8,9},{9,8},{10,11... | collective-permute-start | bytes 10616840 | tf_op jit(solution)/shard_map/ppermute | solution.py:116
  1.2 23.5 %collective-permute-start.10 = (bf16[384,1536]{1,0:T(8,128)(2,1)}, bf16[384,1536]{1,0:T(8,128)(2,1)S(1)}, u32[]{:S(2)}, u32[]{:S(2)}) collective-permute-start(bf16[384,1536]{1,0:T(8,128)(2,1)} %refs_1_.1), channel_id=1, source_target_pairs={{0,1},{1,0},{2,3},{3,2},{4,5},{5,4},{6,7},{7,6},{8,9},{9,8},{10,11... | collective-permute-start | bytes 3538952 | tf_op jit(solution)/shard_map/ppermute | solution.py:116
  1.3 29.3 %collective-permute-start.12 = (bf16[2,1536,256]{2,1,0:T(8,128)(2,1)}, bf16[2,1536,256]{2,1,0:T(8,128)(2,1)S(1)}, u32[]{:S(2)}, u32[]{:S(2)}) collective-permute-start(bf16[2,1536,256]{2,1,0:T(8,128)(2,1)} %refs_11_.1), channel_id=1, source_target_pairs={{0,1},{1,0},{2,3},{3,2},{4,5},{5,4},{6,7},{7,6},{8,9},{9,8},{10,11... | collective-permute-start | bytes 4718600 | tf_op jit(solution)/shard_map/ppermute | solution.py:116
  2.6 5.2 %collective-permute-start.1 = (bf16[16,1536]{1,0:T(8,128)(2,1)S(1)}, bf16[16,1536]{1,0:T(8,128)(2,1)S(1)}, u32[]{:S(2)}, u32[]{:S(2)}) collective-permute-start(bf16[16,1536]{1,0:T(8,128)(2,1)S(1)} %get-tuple-element.28), channel_id=1, source_target_pairs={{0,4},{4,0},{8,12},{12,8},{1,5},{5,1},{9,13},{13,9},{2,6},{6,2},{1... | collective-permute-start | bytes 147464 | tf_op jit(solution)/shard_map/ppermute | solution.py:116
  5.3 5.9 %collective-permute-start.2 = (bf16[16,1536]{1,0:T(8,128)(2,1)S(1)}, bf16[16,1536]{1,0:T(8,128)(2,1)S(1)}, u32[]{:S(2)}, u32[]{:S(2)}) collective-permute-start(bf16[16,1536]{1,0:T(8,128)(2,1)S(1)} %get-tuple-element.29), channel_id=1, source_target_pairs={{0,12},{4,8},{8,4},{12,0},{1,13},{5,9},{9,5},{13,1},{2,14},{6,10},... | collective-permute-start | bytes 147464 | tf_op jit(solution)/shard_map/ppermute | solution.py:116
  7.8 5.0 %collective-permute-start = (bf16[16,1536]{1,0:T(8,128)(2,1)S(1)}, bf16[16,1536]{1,0:T(8,128)(2,1)S(1)}, u32[]{:S(2)}, u32[]{:S(2)}) collective-permute-start(bf16[16,1536]{1,0:T(8,128)(2,1)S(1)} %get-tuple-element.26), channel_id=1, source_target_pairs={{0,8},{4,12},{8,0},{12,4},{1,9},{5,13},{9,1},{13,5},{2,10},{6,14},... | collective-permute-start | bytes 147464 | tf_op jit(solution)/shard_map/ppermute | solution.py:116
  11.2 4.6 %collective-permute-start.6 = (bf16[16,1536]{1,0:T(8,128)(2,1)S(1)}, bf16[16,1536]{1,0:T(8,128)(2,1)S(1)}, u32[]{:S(2)}, u32[]{:S(2)}) collective-permute-start(bf16[16,1536]{1,0:T(8,128)(2,1)S(1)} %get-tuple-element.30.refs_1_), channel_id=1, source_target_pairs={{0,2},{1,3},{2,0},{3,1},{4,6},{5,7},{6,4},{7,5},{8,10},{9,11},{10,... | collective-permute-start | bytes 147464 | tf_op jit(solution)/shard_map/ppermute | solution.py:116
  12.8 4.2 %collective-permute-start.5 = (bf16[16,1536]{1,0:T(8,128)(2,1)S(1)}, bf16[16,1536]{1,0:T(8,128)(2,1)S(1)}, u32[]{:S(2)}, u32[]{:S(2)}) collective-permute-start(bf16[16,1536]{1,0:T(8,128)(2,1)S(1)} %get-tuple-element.27.refs_0_), channel_id=1, source_target_pairs={{0,2},{1,3},{2,0},{3,1},{4,6},{5,7},{6,4},{7,5},{8,10},{9,11},{10,... | collective-permute-start | bytes 147464 | tf_op jit(solution)/shard_map/ppermute | solution.py:116
  15.8 1.6 %collective-permute-start.4 = (bf16[16,1536]{1,0:T(8,128)(2,1)S(1)}, bf16[16,1536]{1,0:T(8,128)(2,1)S(1)}, u32[]{:S(2)}, u32[]{:S(2)}) collective-permute-start(bf16[16,1536]{1,0:T(8,128)(2,1)S(1)} %get-tuple-element.32), channel_id=1, source_target_pairs={{0,1},{1,0},{2,3},{3,2},{4,5},{5,4},{6,7},{7,6},{8,9},{9,8},{10,11... | collective-permute-start | bytes 147464 | tf_op jit(solution)/shard_map/ppermute | solution.py:116
  16.9 4.0 %collective-permute-start.8 = (bf16[16,1536]{1,0:T(8,128)(2,1)S(1)}, bf16[16,1536]{1,0:T(8,128)(2,1)S(1)}, u32[]{:S(2)}, u32[]{:S(2)}) collective-permute-start(bf16[16,1536]{1,0:T(8,128)(2,1)S(1)} %get-tuple-element.32), channel_id=1, source_target_pairs={{0,3},{1,2},{2,1},{3,0},{4,7},{5,6},{6,5},{7,4},{8,11},{9,10},{10,... | collective-permute-start | bytes 147464 | tf_op jit(solution)/shard_map/ppermute | solution.py:116
  17.4 6.2 %collective-permute-start.3 = (bf16[16,1536]{1,0:T(8,128)(2,1)S(1)}, bf16[16,1536]{1,0:T(8,128)(2,1)S(1)}, u32[]{:S(2)}, u32[]{:S(2)}) collective-permute-start(bf16[16,1536]{1,0:T(8,128)(2,1)S(1)} %get-tuple-element.31), channel_id=1, source_target_pairs={{0,1},{1,0},{2,3},{3,2},{4,5},{5,4},{6,7},{7,6},{8,9},{9,8},{10,11... | collective-permute-start | bytes 147464 | tf_op jit(solution)/shard_map/ppermute | solution.py:116
  20.9 3.7 %collective-permute-start.7 = (bf16[16,1536]{1,0:T(8,128)(2,1)S(1)}, bf16[16,1536]{1,0:T(8,128)(2,1)S(1)}, u32[]{:S(2)}, u32[]{:S(2)}) collective-permute-start(bf16[16,1536]{1,0:T(8,128)(2,1)S(1)} %get-tuple-element.31), channel_id=1, source_target_pairs={{0,3},{1,2},{2,1},{3,0},{4,7},{5,6},{6,5},{7,4},{8,11},{9,10},{10,... | collective-permute-start | bytes 147464 | tf_op jit(solution)/shard_map/ppermute | solution.py:116
  24.7 4.8 %copy-start.1 = (f32[256,7]{0,1:T(8,128)S(1)}, f32[256,7]{0,1:T(8,128)}, u32[]{:S(2)}) copy-start(f32[256,7]{0,1:T(8,128)} %param.14) | copy-start | bytes 21508
  24.7 14.7 %copy-start = (bf16[2,1536,256]{2,1,0:T(8,128)(2,1)S(1)}, bf16[2,1536,256]{2,1,0:T(8,128)(2,1)}, u32[]{:S(2)}) copy-start(bf16[2,1536,256]{2,1,0:T(8,128)(2,1)} %refs_11_.1) | copy-start | bytes 4718596
  28.2 11.2 %collective-permute-start.11 = (bf16[128,1536]{1,0:T(8,128)(2,1)S(1)}, bf16[128,1536]{1,0:T(8,128)(2,1)S(1)}, u32[]{:S(2)}, u32[]{:S(2)}) collective-permute-start(bf16[128,1536]{1,0:T(8,128)(2,1)S(1)} %shard_map.99.refs_8_), channel_id=1, source_target_pairs={{0,2},{2,0},{1,3},{3,1},{4,6},{6,4},{5,7},{7,5},{8,10},{10,8},{9,1... | collective-permute-start | bytes 1179656 | tf_op jit(solution)/shard_map/ppermute | solution.py:116
  29.4 1.2 %collective-permute-start.13 = (f32[7,256]{1,0:T(8,128)S(1)}, f32[7,256]{1,0:T(8,128)S(1)}, u32[]{:S(2)}, u32[]{:S(2)}) collective-permute-start(f32[7,256]{1,0:T(8,128)S(1)} %bitcast.12), channel_id=1, source_target_pairs={{0,1},{1,0},{2,3},{3,2},{4,5},{5,4},{6,7},{7,6},{8,9},{9,8},{10,11... | collective-permute-start | bytes 21512 | tf_op jit(solution)/shard_map/ppermute | solution.py:116
  40.6 4.6 %collective-permute-start.14 = (bf16[32,1536]{1,0:T(8,128)(2,1)S(1)}, bf16[32,1536]{1,0:T(8,128)(2,1)S(1)}, u32[]{:S(2)}, u32[]{:S(2)}) collective-permute-start(bf16[32,1536]{1,0:T(8,128)(2,1)S(1)} %get-tuple-element.40), channel_id=1, source_target_pairs={{0,1},{1,0},{2,3},{3,2},{4,5},{5,4},{6,7},{7,6},{8,9},{9,8},{10,11... | collective-permute-start | bytes 294920 | tf_op jit(solution)/shard_map/ppermute | solution.py:116
  40.6 1.9 %collective-permute-start.15 = (f32[16,128]{1,0:T(8,128)S(1)}, f32[16,128]{1,0:T(8,128)S(1)}, u32[]{:S(2)}, u32[]{:S(2)}) collective-permute-start(f32[16,128]{1,0:T(8,128)S(1)} %get-tuple-element.41.refs_0_), channel_id=1, source_target_pairs={{0,1},{1,0},{2,3},{3,2},{4,5},{5,4},{6,7},{7,6},{8,9},{9,8},{10,11... | collective-permute-start | bytes 24584 | tf_op jit(solution)/shard_map/ppermute | solution.py:116
  41.1 3.7 %collective-permute-start.16 = (f32[16,128]{1,0:T(8,128)S(1)}, f32[16,128]{1,0:T(8,128)S(1)}, u32[]{:S(2)}, u32[]{:S(2)}) collective-permute-start(f32[16,128]{1,0:T(8,128)S(1)} %get-tuple-element.41.refs_0_), channel_id=1, source_target_pairs={{0,2},{1,3},{2,0},{3,1},{4,6},{5,7},{6,4},{7,5},{8,10},{9,11},{10,... | collective-permute-start | bytes 24584 | tf_op jit(solution)/shard_map/ppermute | solution.py:116
  42.1 3.1 %collective-permute-start.17 = (f32[16,128]{1,0:T(8,128)S(1)}, f32[16,128]{1,0:T(8,128)S(1)}, u32[]{:S(2)}, u32[]{:S(2)}) collective-permute-start(f32[16,128]{1,0:T(8,128)S(1)} %get-tuple-element.41.refs_0_), channel_id=1, source_target_pairs={{0,3},{1,2},{2,1},{3,0},{4,7},{5,6},{6,5},{7,4},{8,11},{9,10},{10,... | collective-permute-start | bytes 24584 | tf_op jit(solution)/shard_map/ppermute | solution.py:116
  45.3 4.5 %collective-permute-start.18 = (bf16[16,1664]{1,0:T(8,128)(2,1)S(1)}, bf16[16,1664]{1,0:T(8,128)(2,1)S(1)}, u32[]{:S(2)}, u32[]{:S(2)}) collective-permute-start(bf16[16,1664]{1,0:T(8,128)(2,1)S(1)} %get-tuple-element.43), channel_id=1, source_target_pairs={{0,4},{4,0},{8,12},{12,8},{1,5},{5,1},{9,13},{13,9},{2,6},{6,2},{1... | collective-permute-start | bytes 159752 | tf_op jit(solution)/shard_map/ppermute | solution.py:116
  46.8 6.3 %collective-permute-start.19 = (bf16[16,1664]{1,0:T(8,128)(2,1)S(1)}, bf16[16,1664]{1,0:T(8,128)(2,1)S(1)}, u32[]{:S(2)}, u32[]{:S(2)}) collective-permute-start(bf16[16,1664]{1,0:T(8,128)(2,1)S(1)} %get-tuple-element.44), channel_id=1, source_target_pairs={{0,8},{4,12},{8,0},{12,4},{1,9},{5,13},{9,1},{13,5},{2,10},{6,14},... | collective-permute-start | bytes 159752 | tf_op jit(solution)/shard_map/ppermute | solution.py:116
  49.8 5.9 %collective-permute-start.20 = (bf16[16,1664]{1,0:T(8,128)(2,1)S(1)}, bf16[16,1664]{1,0:T(8,128)(2,1)S(1)}, u32[]{:S(2)}, u32[]{:S(2)}) collective-permute-start(bf16[16,1664]{1,0:T(8,128)(2,1)S(1)} %get-tuple-element.45), channel_id=1, source_target_pairs={{0,12},{4,8},{8,4},{12,0},{1,13},{5,9},{9,5},{13,1},{2,14},{6,10},... | collective-permute-start | bytes 159752 | tf_op jit(solution)/shard_map/ppermute | solution.py:116
